TPU v7x, 256 devices: a whole 4x4x8 slice. The times are simulated.
256 devices in a mesh: row: 4 (over x), col: 64 (over y, z, core).
Axes of the slice: x: 4, y: 4, z: 8, core: 2. Of those that a mesh axis runs over, the one named last changes fastest.
Arguments:
- activations: bfloat16 [8, 256, 8192], P('row')
- out_grads: bfloat16 [8, 256, 28672], P('row', None, 'col')
- valid_len: int32 [8], P('row'), may hold values from 1 to 256, 1024 in all
- weight: bfloat16 [8192, 28672], P('row', 'col'), may hold values from -0.0625 to 0.0625
- sketch: bfloat16 [28672, 512], P('col'), may hold values from -6 to 6
Outputs:
- basis: float32 [8192, 512], P(('row', 'col'))
- coeffs: float32 [512, 28672], P('row', 'col')
Inputs may be any that keep to these rules, and one draw needn't show every extreme that they name: `valid_len`: valid tokens of each sequence; at least one sequence fills all 256 slots.
All inputs are finite; a program needn't handle non-finite values. No bound on the sum of `valid_len` on one device may be relied on, other than what follows from the above.
Results may differ from a plain program's by a relative error of at most 0.01.
Values may be sent and summed in bfloat16 or wider, within the bound.
A program may use at most 64 MiB of HBM per device.

v0:
```python
import math

import jax
import jax.numpy as jnp
from jax import lax
from jax.sharding import PartitionSpec as P


def contract_rows(left, right):
    return lax.dot_general(
        left, right, (((0,), (0,)), ((), ())), preferred_element_type=jnp.float32
    )


def gram_local(sketch_rows):
    return lax.dot_general(
        sketch_rows, sketch_rows, (((0,), (0,)), ((), ())), precision=lax.Precision.HIGHEST
    )


def solve_basis(gram, sketch_rows):
    factor_low = jnp.linalg.cholesky(gram)
    return lax.linalg.triangular_solve(
        factor_low, sketch_rows, left_side=False, lower=True, transpose_a=True
    )


def orthonormal_shared(sketch_rows):
    gram = lax.psum(gram_local(sketch_rows), ("row", "col"))
    return solve_basis(gram, sketch_rows)


def reduce_sketch(left, right):
    return lax.psum_scatter(
        jnp.dot(left, right, preferred_element_type=jnp.float32),
        "col",
        scatter_dimension=0,
        tiled=True,
    )


def local(activations, out_grads, valid_len, weight, sketch):
    seq_dev, length, model_width = activations.shape
    rows_here, cols_here = weight.shape
    col_count = lax.axis_size("col")
    col_index = lax.axis_index("col")
    row_index = lax.axis_index("row")
    own_rows = rows_here // col_count
    own_start = col_index * own_rows
    positions = lax.iota(jnp.int32, length)
    raw_sketch = reduce_sketch(weight, sketch)
    partial_mass = jnp.zeros((model_width,), jnp.float32)
    for seq_index in range(seq_dev):
        valid = (positions < valid_len[seq_index]).astype(jnp.bfloat16)
        grad_block = contract_rows(activations[seq_index], out_grads[seq_index] * valid[:, None])
        partial_mass = partial_mass + jnp.sum(grad_block * grad_block, axis=1)
    fisher = lax.psum(partial_mass, ("row", "col"))
    total_mass = jnp.sum(fisher)
    own_mass = lax.dynamic_slice_in_dim(fisher, row_index * rows_here, rows_here, 0)
    row_scale = jnp.sqrt(own_mass / (total_mass / model_width + 1e-06))
    first_sketch = (
        lax.dynamic_slice_in_dim(row_scale, own_start, own_rows, 0)[:, None] * raw_sketch
    ).astype(jnp.bfloat16)
    scaled = (row_scale[:, None] * weight.astype(jnp.float32)).astype(jnp.bfloat16)
    proj_part = contract_rows(scaled, lax.all_gather(first_sketch, "col", axis=0, tiled=True))
    projected = lax.psum(proj_part, "row").astype(jnp.bfloat16)
    second_sketch = reduce_sketch(scaled, projected)
    second_basis = orthonormal_shared(second_sketch)
    group_second = lax.all_gather(second_basis.astype(jnp.bfloat16), "col", axis=0, tiled=True)
    coeff_raw = lax.psum_scatter(
        contract_rows(group_second, scaled).astype(jnp.bfloat16),
        "row",
        scatter_dimension=0,
        tiled=True,
    ).astype(jnp.float32)
    return (second_basis * math.sqrt(model_width), coeff_raw * math.sqrt(cols_here * col_count))


def solution(mesh):
    placed = (
        P("row", None, None),
        P("row", None, "col"),
        P("row"),
        P("row", "col"),
        P("col", None),
    )
    return jax.shard_map(
        local,
        mesh=mesh,
        in_specs=placed,
        out_specs=(P(("row", "col"), None), P("row", "col")),
        check_vma=False,
    )
```

profile of v0, /device:TPU:6, one launch (start us, length us, event | category | flops | bytes accessed | tf_op | source)
XLA Modules:
  0.0 950.6 jit_solution(8031663152801272860)
XLA Ops:
  8.2 4.7 fusion.51
  15.5 4.3 multiply_reduce_fusion
  19.8 4.4 multiply_reduce_fusion.1
  24.2 79.3 %psum.21 = f32[8192]{0:T(1024)S(1)} all-reduce(f32[8192]{0:T(1024)S(1)} %add.64), channel_id=1, replica_groups=mesh['row'=4,'col'=64] {'row','col'}, use_global_device_ids=true, to_apply=%region_2.0 | all-reduce | flops 8192 | bytes 65536 | tf_op jit(solution)/shard_map/psum | solution.py:57
  104.9 55.7 %reduce-scatter.6.cloned.1.call-done = f32[32,512]{1,0:T(8,128)} async-done(((f32[2048,512]{1,0:T(8,128)}), f32[32,512]{1,0:T(8,128)}) %reduce-scatter.6.cloned.1.call-update) | async-done | bytes 65552 | tf_op jit(solution)/shard_map/reduce_scatter | solution.py:34
  162.2 77.8 %all-gather.3.cloned.1.call-done = bf16[2048,512]{1,0:T(8,128)(2,1)} async-done(((bf16[32,512]{1,0:T(8,128)(2,1)}), bf16[2048,512]{1,0:T(8,128)(2,1)}) %all-gather.3.cloned.1.call-update) | async-done | bytes 2097168 | tf_op jit(solution)/shard_map/all_gather | solution.py:65
  240.0 3.6 fusion.6
  243.6 27.1 %all-reduce.5 = bf16[448,512]{1,0:T(8,128)(2,1)S(1)} all-reduce(f32[448,512]{1,0:T(8,128)} %fusion.6), channel_id=1, replica_groups=mesh['row'=4,'col'=64] {'row'}, use_global_device_ids=true, to_apply=%region_5.0 | all-reduce | flops 229376 | bytes 1376256 | tf_op jit(solution)/shard_map/psum | solution.py:66
  270.7 3.2 fusion.5
  274.0 141.6 %reduce-scatter.8.cloned.1.call-done = f32[32,512]{1,0:T(8,128)} async-done(((f32[2048,512]{1,0:T(8,128)}), f32[32,512]{1,0:T(8,128)}) %reduce-scatter.8.cloned.1.call-update) | async-done | bytes 65552 | tf_op jit(solution)/shard_map/reduce_scatter | solution.py:34
  415.6 3.0 fusion.52
  419.3 258.8 %all-reduce.4.cloned.1.call-done = f32[512,512]{0,1:T(8,128)} async-done(((f32[512,512]{0,1:T(8,128)}), f32[512,512]{0,1:T(8,128)}) %all-reduce.4.cloned.1.call-update) | async-done | bytes 1048592 | tf_op jit(solution)/shard_map/psum | solution.py:29
  682.2 11.7 %cholesky.104 = f32[128,128]{1,0:T(8,128)S(1)} custom-call(f32[128,128]{1,0:T(8,128)S(1)} %cholesky.266), custom_call_target="Cholesky" | custom-call | tf_op jit(solution)/shard_map/jit(cholesky)/cholesky | solution.py:22
  694.1 9.8 %custom-call.30 = f32[1,128,128]{1,2,0:T(8,128)S(1)} custom-call(f32[1,128,128]{2,1,0:T(8,128)S(1)} %get-tuple-element.29), custom_call_target="InvertDiagBlocksLowerTriangular" | custom-call | tf_op jit(solution)/shard_map/jit(cholesky)/cholesky | solution.py:22
  707.0 13.2 %cholesky.217 = f32[128,128]{1,0:T(8,128)} custom-call(f32[128,128]{1,0:T(8,128)} %cholesky.270), custom_call_target="Cholesky" | custom-call | tf_op jit(solution)/shard_map/jit(cholesky)/cholesky | solution.py:22
  721.7 11.5 %custom-call.31 = f32[1,128,128]{1,2,0:T(8,128)} custom-call(f32[1,128,128]{2,1,0:T(8,128)} %get-tuple-element.26), custom_call_target="InvertDiagBlocksLowerTriangular" | custom-call | tf_op jit(solution)/shard_map/jit(cholesky)/cholesky | solution.py:22
  736.2 13.2 %cholesky.238 = f32[128,128]{1,0:T(8,128)} custom-call(f32[128,128]{1,0:T(8,128)} %cholesky.275), custom_call_target="Cholesky" | custom-call | tf_op jit(solution)/shard_map/jit(cholesky)/cholesky | solution.py:22
  751.6 11.3 %custom-call.32 = f32[1,128,128]{1,2,0:T(8,128)} custom-call(f32[1,128,128]{2,1,0:T(8,128)} %get-tuple-element.23), custom_call_target="InvertDiagBlocksLowerTriangular" | custom-call | tf_op jit(solution)/shard_map/jit(cholesky)/cholesky | solution.py:22
  765.1 11.7 %cholesky.255 = f32[128,128]{1,0:T(8,128)S(1)} custom-call(f32[128,128]{1,0:T(8,128)S(1)} %convolution_subtract_fusion.2), custom_call_target="Cholesky" | custom-call | tf_op jit(solution)/shard_map/jit(cholesky)/cholesky | solution.py:22
  782.7 14.0 %while.1 = (s32[]{:T(128)}, f32[512,512]{1,0:T(8,128)}, s32[4,2]{0,1:T(2,128)S(1)}, f32[4,128,128]{2,1,0:T(8,128)}, s32[]{:T(128)}) while((s32[]{:T(128)}, f32[512,512]{1,0:T(8,128)}, s32[4,2]{0,1:T(2,128)S(1)}, f32[4,128,128]{2,1,0:T(8,128)}, s32[]{:T(128)}) %tuple.32), condition=%wide.while_cond, body=%wide.while_body.sunk | while | flops 2 | bytes 132705 | solution.py:23
  783.3 2.9 bitcast_dynamic-update-slice_fusion.2
  796.7 40.1 %custom-call.33 = f32[4,128,128]{1,2,0:T(8,128)S(1)} custom-call(f32[4,128,128]{2,1,0:T(8,128)} %get-tuple-element.9), custom_call_target="InvertDiagBlocksLowerTriangular" | custom-call | tf_op jit(solution)/shard_map/triangular_solve | solution.py:23
  841.7 76.5 %all-gather.5.cloned.1.call-done = bf16[2048,512]{1,0:T(8,128)(2,1)} async-done(((bf16[32,512]{1,0:T(8,128)(2,1)}), bf16[2048,512]{1,0:T(8,128)(2,1)}) %all-gather.5.cloned.1.call-update) | async-done | bytes 2097168 | tf_op jit(solution)/shard_map/all_gather | solution.py:69
  922.5 19.0 %reduce-scatter.10.cloned.1.call-done = bf16[128,448]{1,0:T(8,128)(2,1)} async-done(((bf16[512,448]{1,0:T(8,128)(2,1)}), bf16[128,448]{1,0:T(8,128)(2,1)}) %reduce-scatter.10.cloned.1.call-update) | async-done | bytes 114704
  (79 shorter events, 48.1 us)
Async XLA Ops:
  7.2 1.0 copy-start
  7.2 153.4 %reduce-scatter.6.cloned.1.call-start = ((), (), s32[]{:S(2)}) async-start(), calls=%async_computation.3 | async-start | bytes 4259840 | tf_op jit(solution)/shard_map/reduce_scatter | solution.py:34
  12.9 0.7 copy-start.4
  12.9 2.6 copy-start.5
  12.9 227.0 %all-gather.3.cloned.1.call-start = ((), (), s32[]{:S(2)}) async-start(), calls=%async_computation.4 | async-start | bytes 2129920 | tf_op jit(solution)/shard_map/all_gather | solution.py:65
  19.8 220.2 %copy-start.1 = (bf16[2048,448]{0,1:T(8,128)(2,1)S(1)}, bf16[2048,448]{0,1:T(8,128)(2,1)}, u32[]{:S(2)}) copy-start(bf16[2048,448]{0,1:T(8,128)(2,1)} %param.8) | copy-start | bytes 5505028
  162.2 253.4 %reduce-scatter.8.cloned.1.call-start = ((), (), s32[]{:S(2)}) async-start(), calls=%async_computation.5 | async-start | bytes 4259840 | tf_op jit(solution)/shard_map/reduce_scatter | solution.py:34
  273.9 404.2 %all-reduce.4.cloned.1.call-start = ((), (), s32[]{:S(2)}) async-start(), calls=%async_computation.6 | async-start | bytes 2097152 | tf_op jit(solution)/shard_map/psum | solution.py:29
  418.6 499.6 %all-gather.5.cloned.1.call-start = ((), (), s32[]{:S(2)}) async-start(), calls=%async_computation.7 | async-start | bytes 2129920 | tf_op jit(solution)/shard_map/all_gather | solution.py:69
  681.2 1.0 copy-start.2
  734.2 102.5 %copy-start.3 = (f32[32,512]{1,0:T(8,128)S(1)}, f32[32,512]{1,0:T(8,128)}, u32[]{:S(2)}) copy-start(f32[32,512]{1,0:T(8,128)} %reduce-scatter.8.cloned.1.call-done) | copy-start | bytes 196612
  841.6 100.0 %reduce-scatter.10.cloned.1.call-start = ((), (), s32[]{:S(2)}) async-start(), calls=%async_computation.8 | async-start | bytes 655360
Sparse Core Ops, SparseCore 0:
  13.1 147.5 reduce-scatter.5
  164.0 75.9 all-gather.2
  274.0 141.5 reduce-scatter.7
  420.9 257.2 all-reduce.3
  841.7 76.3 all-gather.4
  922.0 19.5 reduce-scatter.9
where the time goes:
time: 961 us; the launch traced here: 951 us
  waiting for transfers between devices  630 us (66%)
  other arithmetic  136 us (14%)
  blocking collectives  106 us (11%)
  matrix products  37.2 us (4%)
  local copies, waits for them, and re-layouts  22.7 us (2%)
  between operations  18 us (2%)
    psum x1, waiting for transfers between devices, orthonormal_shared(): gram = lax.psum(gram_local(sketch_rows), ('row', 'col'))  259 us
    reduce_scatter x2, waiting for transfers between devices, reduce_sketch(): lax.psum_scatter(jnp.dot(left, right, preferred_element_type=jnp.float32)...  197 us
    another operation x14, other arithmetic, solve_basis(): factor_low = jnp.linalg.cholesky(gram)  87.4 us
    psum x1, blocking collectives, local(): fisher = lax.psum(partial_mass, ('row', 'col'))  79.3 us
    all_gather x1, waiting for transfers between devices, local(): lax.all_gather(first_sketch, 'col', axis=0, tiled=True)  77.8 us
    all_gather x1, waiting for transfers between devices, local(): lax.all_gather(second_basis.astype(jnp.bfloat16), 'col', axis=0, tiled=True)  76.5 us
    another operation x3, other arithmetic, solve_basis(): lax.linalg.triangular_solve(factor_low, sketch_rows, left_side=False, low...  42 us
    psum x1, blocking collectives, local(): projected = lax.psum(proj_part, 'row').astype(jnp.bfloat16)  27.1 us
  transfers between devices with their start and end apart: 6, of which 6 were waited for; matrix products, arithmetic and copies ran while one was open for 1% of the time, Pallas kernels for 0%

commit v1 on v0

v1 whole, which is shorter than its diff:
```python
import functools
import math

import jax
import jax.numpy as jnp
from jax import lax
from jax.experimental import pallas as pl
from jax.experimental.pallas import tpu as pltpu
from jax.sharding import PartitionSpec as P

MESH = pl.DeviceIdType.MESH
VMEM = pl.BlockSpec(memory_space=pltpu.VMEM)
F32, BF16 = jnp.float32, jnp.bfloat16
ROWS, COLS, RANK, DIM, FF = 2048, 448, 512, 8192, 28672
HALF, YCH, ZCH = 1024, 256, 32
PIECES = 4
WIDE = RANK // PIECES
ZTYPE = F32


def f32(ref):
    return ref[...].astype(F32)


def at_rows(ref, start, count, step=16):
    return ref.at[pl.ds(pl.multiple_of(start, step), count)]


class Net:
    def __init__(self, send_sems, recv_sems):
        self.send_sems, self.recv_sems, self.copies = send_sems, recv_sems, []

    def send(self, src, dst, device):
        slot = len(self.copies)
        copy = pltpu.make_async_remote_copy(
            src_ref=src,
            dst_ref=dst,
            send_sem=self.send_sems.at[slot],
            recv_sem=self.recv_sems.at[slot],
            device_id=device,
            device_id_type=MESH,
        )
        copy.start()
        self.copies.append(copy)
        return copy

    def drain(self):
        for copy in self.copies:
            copy.wait_send()


def greet(peers):
    barrier = pltpu.get_barrier_semaphore()
    for peer in peers:
        pl.semaphore_signal(barrier, inc=1, device_id=peer, device_id_type=MESH)
    pl.semaphore_wait(barrier, len(peers))


def place():
    row, col = lax.axis_index("row"), lax.axis_index("col")
    return row, col, lax.rem(col, 2), lax.rem(col // 2, 8), col // 16


class Ring:
    def __init__(self, net, me, up, down, chunk, front):
        self.net, self.up, self.down, self.front, self.back = net, up, down, front, chunk - front
        self.own = me * chunk
        self.next = lax.rem(me + 1, 4) * chunk
        self.far = lax.rem(me + 2, 4) * chunk
        self.last = lax.rem(me + 3, 4) * chunk

    def reduce_start(self, src, got_f, got_b):
        send, front, back = self.net.send, self.front, self.back
        self.red = [
            send(src(self.far, front), got_f.at[0], self.up),
            send(src(self.far + front, back), got_b.at[0], self.down),
            send(src(self.next + front, back), got_b.at[1], self.up),
            send(src(self.last, front), got_f.at[1], self.down),
        ]

    def reduce_relay(self, src, got_f, got_b, sum_f, sum_b):
        send, front, back = self.net.send, self.front, self.back
        self.red[0].wait_recv()
        sum_f[...] = (f32(got_f.at[0]) + f32(src(self.next, front))).astype(sum_f.dtype)
        self.red.append(send(sum_f, got_f.at[2], self.up))
        self.red[1].wait_recv()
        sum_b[...] = (f32(got_b.at[0]) + f32(src(self.last + front, back))).astype(sum_b.dtype)
        self.red.append(send(sum_b, got_b.at[2], self.down))

    def reduce_end(self, src, got_f, got_b):
        for copy in self.red[2:]:
            copy.wait_recv()
        top = f32(src(self.own, self.front)) + f32(got_f.at[1]) + f32(got_f.at[2])
        low = f32(src(self.own + self.front, self.back)) + f32(got_b.at[1]) + f32(got_b.at[2])
        return top, low

    def gather_start(self, dst):
        whole = dst(self.own, self.front + self.back)
        self.gat = [self.net.send(whole, whole, self.up), self.net.send(whole, whole, self.down)]

    def gather_relay(self, dst):
        self.gat[0].wait_recv()
        part = dst(self.last, self.front)
        self.gat.append(self.net.send(part, part, self.up))
        self.gat[1].wait_recv()
        part = dst(self.next + self.front, self.back)
        self.gat.append(self.net.send(part, part, self.down))

    def gather_end(self):
        self.gat[2].wait_recv()
        self.gat[3].wait_recv()


def col_sum_steps(net, x_ref, o_ref, scale_ref, square, pair, mine, got_f, got_b, sum_f, sum_b, ysum, zgot):
    row, _, core, z, y = place()

    def at(yy, zz, kk):
        return (row, (yy * 8 + zz) * 2 + kk)

    partner = at(y, z, 1 - core)
    up, down = at(lax.rem(y + 1, 4), z, core), at(lax.rem(y + 3, 4), z, core)
    zpeer = [at(y, lax.rem(z + d, 8), core) for d in range(1, 8)]
    base, other = core * HALF, (1 - core) * HALF
    state = [dict() for _ in range(PIECES)]

    def cols(p):
        return pl.ds(p * WIDE, WIDE)

    def out(p, start, count):
        return o_ref.at[pl.ds(pl.multiple_of(base + start, 16), count), cols(p)]

    def src(p):
        return lambda start, count: mine.at[p, pl.ds(pl.multiple_of(start, 16), count)]

    def own_scale():
        start = base + y * YCH + z * ZCH
        line = scale_ref[pl.ds(start // 128, 1), :]
        lanes = lax.broadcasted_iota(jnp.int32, (ZCH, 128), 1)
        rows = lax.broadcasted_iota(jnp.int32, (ZCH, 128), 0)
        picked = jnp.where(lanes == rows + lax.rem(start, 128), line, 0.0)
        scale = jnp.sum(picked, axis=1, keepdims=True)
        return scale * scale if square else scale

    def s0(p):
        half = x_ref.at[pl.ds(pl.multiple_of(other, 16), HALF), cols(p)]
        state[p]["pair"] = net.send(half, pair.at[p], partner)

    def s1(p):
        state[p]["pair"].wait_recv()
        own = x_ref.at[pl.ds(pl.multiple_of(base, 16), HALF), cols(p)]
        mine[p] = (f32(own) + f32(pair.at[p])).astype(BF16)
        ring = Ring(net, y, up, down, YCH, YCH // 2)
        state[p]["ring"] = ring
        ring.reduce_start(src(p), got_f.at[p], got_b.at[p])

    def s2(p):
        state[p]["ring"].reduce_relay(src(p), got_f.at[p], got_b.at[p], sum_f.at[p], sum_b.at[p])

    def s3(p):
        top, low = state[p]["ring"].reduce_end(src(p), got_f.at[p], got_b.at[p])
        ysum[p, pl.ds(0, YCH // 2)] = top.astype(ZTYPE)
        ysum[p, pl.ds(YCH // 2, YCH // 2)] = low.astype(ZTYPE)
        state[p]["z"] = []
        for d in range(1, 8):
            part = ysum.at[p, pl.ds(pl.multiple_of(lax.rem(z + d, 8) * ZCH, 16), ZCH)]
            state[p]["z"].append(net.send(part, zgot.at[p, d - 1], zpeer[d - 1]))

    def s4(p):
        total = f32(ysum.at[p, pl.ds(pl.multiple_of(z * ZCH, 16), ZCH)])
        for d in range(7):
            state[p]["z"][d].wait_recv()
            total = total + f32(zgot.at[p, d])
        part = out(p, y * YCH + z * ZCH, ZCH)
        part[...] = (total * own_scale()).astype(BF16)
        state[p]["g"] = [net.send(part, part, peer) for peer in zpeer]

    def s5(p):
        for copy in state[p]["g"]:
            copy.wait_recv()
        ring = state[p]["ring"]
        ring.gather_start(functools.partial(out, p))
        whole = out(p, ring.own, YCH)
        state[p]["c"] = [net.send(whole, whole, partner)]

    def s6(p):
        ring = state[p]["ring"]
        ring.gather_relay(functools.partial(out, p))
        for start in (ring.last, ring.next):
            whole = out(p, start, YCH)
            state[p]["c"].append(net.send(whole, whole, partner))

    def s7(p):
        ring = state[p]["ring"]
        ring.gather_end()
        whole = out(p, ring.far, YCH)
        state[p]["c"].append(net.send(whole, whole, partner))

    def s8(p):
        for copy in state[p]["c"]:
            copy.wait_recv()

    return [s0, s1, s2, s3, s4, s5, s6, s7, s8], [partner, up, down] + zpeer


COL_COPIES = PIECES * 29
COL_SCRATCH = [
    pltpu.VMEM((PIECES, HALF, WIDE), F32),
    pltpu.VMEM((PIECES, HALF, WIDE), BF16),
    pltpu.VMEM((PIECES, 3, YCH // 2, WIDE), BF16),
    pltpu.VMEM((PIECES, 3, YCH // 2, WIDE), BF16),
    pltpu.VMEM((PIECES, YCH // 2, WIDE), BF16),
    pltpu.VMEM((PIECES, YCH // 2, WIDE), BF16),
    pltpu.VMEM((PIECES, YCH, WIDE), ZTYPE),
    pltpu.VMEM((PIECES, 7, ZCH, WIDE), ZTYPE),
]


ORDER = (0.0, 2.5, 5.0, 7.5, 14.0, 19.0, 22.0, 24.5, 26.0)
GAPS = (0.1, 1.8, 2.2, 2.2, 4.0, 4.0, 4.0, 4.0, 4.0)


def run_steps(steps, extra=()):
    events = [(ORDER[s] + GAPS[s] * p, s, p) for s in range(len(steps)) for p in range(PIECES)]
    events += [(when, -1, n) for n, (when, _) in enumerate(extra)]
    for _, s, n in sorted(events):
        if s < 0:
            extra[n][1]()
        else:
            steps[s](n)


def col_sum_kernel(x_ref, scale_ref, o_ref, send_sems, recv_sems, *scratch):
    net = Net(send_sems, recv_sems)
    steps, peers = col_sum_steps(net, x_ref, o_ref, scale_ref, False, *scratch)
    greet(peers)
    run_steps(steps)
    net.drain()


def first_kernel(x_ref, f_ref, o_ref, scale_ref, send_sems, recv_sems, fx, f1, fc, f2, fy, f3, fz, ft, fg, *scratch):
    net = Net(send_sems, recv_sems)
    steps, peers = col_sum_steps(net, x_ref, o_ref, scale_ref, True, *scratch)
    row, col, core, z, y = place()
    xpeer = [(lax.rem(row + d, 4), col) for d in range(1, 4)]
    far = (row, (lax.rem(y + 2, 4) * 8 + z) * 2 + core)
    ypeer = [peers[1], far, peers[2]]
    state = {}

    def t0():
        state["x"] = [
            net.send(at_rows(f_ref, lax.rem(row + d, 4) * 16, 16, 8), fx.at[d - 1], xpeer[d - 1])
            for d in range(1, 4)
        ]

    def t1():
        for copy in state["x"]:
            copy.wait_recv()
        f1[...] = at_rows(f_ref, row * 16, 16, 8)[...] + fx[0] + fx[1] + fx[2]
        state["c"] = net.send(f1, fc, peers[0])

    def t2():
        state["c"].wait_recv()
        f2[...] = f1[...] + fc[...]
        state["y"] = [net.send(f2, fy.at[d], ypeer[d]) for d in range(3)]

    def t3():
        for copy in state["y"]:
            copy.wait_recv()
        f3[...] = f2[...] + fy[0] + fy[1] + fy[2]
        state["z"] = [net.send(f3, fz.at[d], peers[3 + d]) for d in range(7)]

    def t4():
        total = f3[...]
        for d in range(7):
            state["z"][d].wait_recv()
            total = total + fz[d]
        scale_ref[...] = total
        ft[...] = total[0:8] + total[8:16]
        state["t"] = [net.send(ft, fg.at[d], xpeer[d]) for d in range(3)]

    def t5():
        for copy in state["t"]:
            copy.wait_recv()
        mass = jnp.sum(ft[...] + fg[0] + fg[1] + fg[2], keepdims=True)
        scale_ref[...] = jnp.sqrt(scale_ref[...] / (mass / DIM + 1e-06))

    greet(peers + [far] + xpeer)
    run_steps(steps, ((-1.0, t0), (2.6, t1), (3.9, t2), (7.0, t3), (11.5, t4), (13.9, t5)))
    net.drain()


def params(collective_id, mib):
    return pltpu.CompilerParams(
        collective_id=collective_id, has_side_effects=True, vmem_limit_bytes=mib << 20
    )


def first_sums(raw, mass):
    piece = (16, 128)
    return pl.pallas_call(
        first_kernel,
        out_shape=(jax.ShapeDtypeStruct((ROWS, RANK), BF16), jax.ShapeDtypeStruct(piece, F32)),
        in_specs=[VMEM, VMEM],
        out_specs=(VMEM, VMEM),
        scratch_shapes=[
            pltpu.SemaphoreType.DMA((COL_COPIES + 17,)),
            pltpu.SemaphoreType.DMA((COL_COPIES + 17,)),
            pltpu.VMEM((3,) + piece, F32),
            pltpu.VMEM(piece, F32),
            pltpu.VMEM(piece, F32),
            pltpu.VMEM(piece, F32),
            pltpu.VMEM((3,) + piece, F32),
            pltpu.VMEM(piece, F32),
            pltpu.VMEM((7,) + piece, F32),
            pltpu.VMEM((8, 128), F32),
            pltpu.VMEM((3, 8, 128), F32),
        ]
        + COL_SCRATCH,
        compiler_params=params(0, 28),
        name="first_sums",
    )(raw, mass)


def col_sum(x, scale):
    return pl.pallas_call(
        col_sum_kernel,
        out_shape=jax.ShapeDtypeStruct((ROWS, RANK), BF16),
        in_specs=[VMEM, VMEM],
        out_specs=VMEM,
        scratch_shapes=[
            pltpu.SemaphoreType.DMA((COL_COPIES,)),
            pltpu.SemaphoreType.DMA((COL_COPIES,)),
        ]
        + COL_SCRATCH,
        compiler_params=params(1, 28),
        name="col_sum",
    )(x, scale)


def ring_scratch(copies, front, back, width, dtype):
    return [
        pltpu.SemaphoreType.DMA((copies,)),
        pltpu.SemaphoreType.DMA((copies,)),
        pltpu.VMEM((3, front, width), dtype),
        pltpu.VMEM((3, back, width), dtype),
        pltpu.VMEM((front, width), dtype),
        pltpu.VMEM((back, width), dtype),
    ]


def row_ring(net, chunk, front):
    row, col, _, _, _ = place()
    up, down = (lax.rem(row + 1, 4), col), (lax.rem(row + 3, 4), col)
    return Ring(net, row, up, down, chunk, front), [up, down]


def row_sum_kernel(x_ref, o_ref, send_sems, recv_sems, got_f, got_b, sum_f, sum_b):
    net = Net(send_sems, recv_sems)
    ring, peers = row_ring(net, 112, 64)
    greet(peers)
    src, dst = functools.partial(at_rows, x_ref), functools.partial(at_rows, o_ref)
    ring.reduce_start(src, got_f, got_b)
    ring.reduce_relay(src, got_f, got_b, sum_f, sum_b)
    top, low = ring.reduce_end(src, got_f, got_b)
    dst(ring.own, 64)[...] = top.astype(BF16)
    dst(ring.own + 64, 48)[...] = low.astype(BF16)
    ring.gather_start(dst)
    ring.gather_relay(dst)
    ring.gather_end()
    net.drain()


def row_sum(x):
    return pl.pallas_call(
        row_sum_kernel,
        out_shape=jax.ShapeDtypeStruct((COLS, RANK), BF16),
        in_specs=[VMEM],
        out_specs=VMEM,
        scratch_shapes=ring_scratch(10, 64, 48, RANK, BF16),
        compiler_params=params(2, 8),
        name="row_sum",
    )(x)


def gram_kernel(y_ref, o_ref, send_sems, recv_sems, got_f, got_b, sum_f, sum_b, own):
    net = Net(send_sems, recv_sems)
    row, col, core, z, y = place()
    partner = (row, (y * 8 + z) * 2 + 1 - core)
    ring, peers = row_ring(net, 64, 32)
    half = core * 256
    left = y_ref[:, pl.ds(pl.multiple_of(half, 128), 256)]
    own[...] = lax.dot_general(left, y_ref[...], (((0,), (0,)), ((), ())), preferred_element_type=F32)
    greet(peers + [partner])
    src = functools.partial(at_rows, own, step=8)

    def dst(start, count):
        return at_rows(o_ref, half + start, count, 8)

    ring.reduce_start(src, got_f, got_b)
    ring.reduce_relay(src, got_f, got_b, sum_f, sum_b)
    top, low = ring.reduce_end(src, got_f, got_b)
    dst(ring.own, 32)[...] = top
    dst(ring.own + 32, 32)[...] = low
    ring.gather_start(dst)
    swaps = [net.send(dst(ring.own, 64), dst(ring.own, 64), partner)]
    ring.gather_relay(dst)
    for start in (ring.last, ring.next):
        swaps.append(net.send(dst(start, 64), dst(start, 64), partner))
    ring.gather_end()
    swaps.append(net.send(dst(ring.far, 64), dst(ring.far, 64), partner))
    for copy in swaps:
        copy.wait_recv()
    net.drain()


def gram_sum(y):
    return pl.pallas_call(
        gram_kernel,
        out_shape=jax.ShapeDtypeStruct((RANK, RANK), F32),
        in_specs=[VMEM],
        out_specs=VMEM,
        scratch_shapes=ring_scratch(14, 32, 32, RANK, F32) + [pltpu.VMEM((256, RANK), F32)],
        compiler_params=params(3, 12),
        name="gram_sum",
    )(y)


def row_scatter_kernel(x_ref, o_ref, send_sems, recv_sems, got_f, got_b, sum_f, sum_b):
    net = Net(send_sems, recv_sems)
    ring, peers = row_ring(net, 1, 1)
    greet(peers)

    def src(where, count):
        return x_ref.at[pl.ds(where[1], count), pl.ds(pl.multiple_of(where[0] * 128, 128), 128)]

    send = net.send
    red = [
        send(src((ring.far, 0), 224), got_f.at[0], ring.up),
        send(src((ring.far, 224), 224), got_b.at[0], ring.down),
        send(src((ring.next, 224), 224), got_b.at[1], ring.up),
        send(src((ring.last, 0), 224), got_f.at[1], ring.down),
    ]
    red[0].wait_recv()
    sum_f[...] = (f32(got_f.at[0]) + f32(src((ring.next, 0), 224))).astype(BF16)
    red.append(send(sum_f, got_f.at[2], ring.up))
    red[1].wait_recv()
    sum_b[...] = (f32(got_b.at[0]) + f32(src((ring.last, 224), 224))).astype(BF16)
    red.append(send(sum_b, got_b.at[2], ring.down))
    for copy in red[2:]:
        copy.wait_recv()
    top = f32(src((ring.own, 0), 224)) + f32(got_f.at[1]) + f32(got_f.at[2])
    low = f32(src((ring.own, 224), 224)) + f32(got_b.at[1]) + f32(got_b.at[2])
    o_ref[pl.ds(0, 224)] = top * math.sqrt(FF)
    o_ref[pl.ds(224, 224)] = low * math.sqrt(FF)
    net.drain()


def row_scatter(x):
    return pl.pallas_call(
        row_scatter_kernel,
        out_shape=jax.ShapeDtypeStruct((COLS, RANK // 4), F32),
        in_specs=[VMEM],
        out_specs=VMEM,
        scratch_shapes=ring_scratch(6, 224, 224, 128, BF16),
        compiler_params=params(4, 8),
        name="row_scatter",
    )(x)


def unit_inverse(block):
    size, group = 128, 8
    count = size // group
    lanes = lax.broadcasted_iota(jnp.int32, (group, size), 1)
    sub = lax.broadcasted_iota(jnp.int32, (group, size), 0)

    def full(x):
        return jnp.broadcast_to(x, (group, size))

    s = [block[group * a : group * a + group] for a in range(count)]
    t = [(lanes == sub + group * a).astype(F32) for a in range(count)]
    for a in range(count):
        lo = a * group
        splat = [[full(s[b][:, lo + m : lo + m + 1]) for b in range(a, count)] for m in range(group)]
        d = [[full(splat[m][0][q : q + 1]) for m in range(group)] for q in range(group)]
        row_s = [full(s[a][q : q + 1]) for q in range(group)]
        row_t = [full(t[a][q : q + 1]) for q in range(group)]
        inv = []
        for m in range(group):
            inv.append(1.0 / d[m][m])
            for q in range(m + 1, group):
                f = d[q][m] * inv[m]
                for w in range(m + 1, group):
                    d[q][w] = d[q][w] - f * d[m][w]
                row_s[q] = row_s[q] - f * row_s[m]
                row_t[q] = row_t[q] - f * row_t[m]
        out = t[a]
        for m in range(group):
            out = jnp.where(sub == m, row_t[m] * jnp.sqrt(inv[m]), out)
        t[a] = out
        for m in reversed(range(group)):
            for q in range(m + 1, group):
                row_s[m] = row_s[m] - d[m][q] * row_s[q]
                row_t[m] = row_t[m] - d[m][q] * row_t[q]
            row_s[m] = row_s[m] * inv[m]
            row_t[m] = row_t[m] * inv[m]
        for b in range(a + 1, count):
            for m in range(group):
                s[b] = s[b] - splat[m][b - a] * row_s[m]
                t[b] = t[b] - splat[m][b - a] * row_t[m]
    return jnp.concatenate(t, axis=0)


def inverse_kernel(g_ref, high_ref, low_ref, x_ref):
    size = 128
    x_ref[...] = g_ref[...]
    eye = lax.broadcasted_iota(jnp.int32, (size, size), 0) == lax.broadcasted_iota(jnp.int32, (size, size), 1)

    def dot(a, b, dims):
        return lax.dot_general(a, b, (dims, ((), ())), precision=lax.Precision.HIGHEST, preferred_element_type=F32)

    def block(k, carry):
        at = pl.ds(pl.multiple_of(k * size, size), size)
        unit = unit_inverse(x_ref[at, at])
        x_ref[:, at] = jnp.zeros((RANK, size), F32)
        x_ref[at, at] = eye.astype(F32)
        line = dot(unit, x_ref[at, :], ((1,), (0,)))
        later = lax.broadcasted_iota(jnp.int32, (size, RANK), 1) >= (k + 1) * size
        done = jnp.where(later, 0.0, line)
        high = done.astype(BF16)
        high_ref[at, :] = high
        low_ref[at, :] = (done - high.astype(F32)).astype(BF16)
        x_ref[...] = x_ref[...] - dot(jnp.where(later, line, 0.0), line, ((0,), (0,)))
        return carry

    lax.fori_loop(0, RANK // size, block, 0)


def inverse_factor(g):
    shape = jax.ShapeDtypeStruct((RANK, RANK), BF16)
    return pl.pallas_call(
        inverse_kernel,
        out_shape=(shape, shape),
        in_specs=[VMEM],
        out_specs=(VMEM, VMEM),
        scratch_shapes=[pltpu.VMEM((RANK, RANK), F32)],
        compiler_params=pltpu.CompilerParams(vmem_limit_bytes=16 << 20),
        name="inverse_factor",
    )(g)


def contract_rows(left, right):
    return lax.dot_general(left, right, (((0,), (0,)), ((), ())), preferred_element_type=F32)


def split_dot(left, right):
    dims = (((1,), (1,)), ((), ()))
    return sum(lax.dot_general(left, term, dims, preferred_element_type=F32) for term in right)


def local(activations, out_grads, valid_len, weight, sketch):
    seq_dev, length, width = activations.shape
    col_index = lax.axis_index("col")
    positions = lax.iota(jnp.int32, length)
    raw = jnp.dot(weight, sketch, preferred_element_type=F32)
    mass = jnp.zeros((width,), F32)
    for seq in range(seq_dev):
        valid = (positions < valid_len[seq]).astype(BF16)
        grad = contract_rows(activations[seq], out_grads[seq] * valid[:, None])
        mass = mass + jnp.sum(grad * grad, axis=1)
    weighted, scale = first_sums(raw, mass.reshape(64, 128))
    projected = row_sum(contract_rows(weight, weighted).astype(BF16))
    second = col_sum(jnp.dot(weight, projected, preferred_element_type=F32), scale)
    scale = scale.reshape(ROWS, 1)
    inverse = inverse_factor(gram_sum(second))
    basis = split_dot(second, inverse)
    own = split_dot(lax.dynamic_slice_in_dim(second, col_index * 32, 32, 0), inverse)
    part = contract_rows(weight, (scale * basis).astype(BF16)).astype(BF16)
    return own * math.sqrt(DIM), row_scatter(part).T


def solution(mesh):
    placed = (
        P("row", None, None),
        P("row", None, "col"),
        P("row"),
        P("row", "col"),
        P("col", None),
    )
    return jax.shard_map(
        local,
        mesh=mesh,
        in_specs=placed,
        out_specs=(P(("row", "col"), None), P("row", "col")),
        check_vma=False,
    )
```

time: 961 us -> 207 us (0.22)
  waiting for transfers between devices: 630 us -> 0 us
  Pallas kernels: 0 us -> 182 us
  other arithmetic: 136 us -> 1.31 us
  blocking collectives: 106 us -> 0 us
  local copies, waits for them, and re-layouts: 22.7 us -> 2.31 us
  matrix products: 37.2 us -> 19.8 us
  between operations: 18 us -> 0.79 us
    psum x1 -> x0, waiting for transfers between devices: 259 us -> none  [orthonormal_shared(): gram = lax.psum(gram_local(sketch_rows), ('row', 'col'))]
    reduce_scatter x2 -> x0, waiting for transfers between devices: 197 us -> none  [reduce_sketch(): lax.psum_scatter(jnp.dot(left, right, preferred_element_type=jnp.float32)...]
    pallas_call x0 -> x6, Pallas kernels: none -> 182 us  [the longest x1 53.8 us: first_sums(): pl.pallas_call(first_kernel, out_shape=(jax.ShapeDtypeStruct((ROWS, RANK)...]
    all_gather x2 -> x0, waiting for transfers between devices: 154 us -> none  [the longest x1 77.8 us: local(): lax.all_gather(first_sketch, 'col', axis=0, tiled=True)]
    another operation x17 -> x0, other arithmetic: 129 us -> none  [the longest x14 87.4 us: solve_basis(): factor_low = jnp.linalg.cholesky(gram)]
    psum x2 -> x0, blocking collectives: 106 us -> none  [the longest x1 79.3 us: local(): fisher = lax.psum(partial_mass, ('row', 'col'))]
    unnamed x7 -> x0, waiting for transfers between devices: 19.1 us -> none
    another operation x17 -> x0, local copies, waits for them, and re-layouts: 16 us -> none
  transfers between devices with their start and end apart: 6 -> 0, of which waited for: 6 -> 0; matrix products, arithmetic and copies ran while one was open for 1% -> 0% of each run, Pallas kernels for 0% -> 0%
where the time goes in v1:
time: 207 us; the launch traced here: 206 us
  Pallas kernels  182 us (88%)
  matrix products  19.8 us (10%)
  local copies, waits for them, and re-layouts  2.31 us (1%)
    pallas_call x1, Pallas kernels, first_sums(): pl.pallas_call(first_kernel, out_shape=(jax.ShapeDtypeStruct((ROWS, RANK)...  53.8 us
    pallas_call x1, Pallas kernels, col_sum(): pl.pallas_call(col_sum_kernel, out_shape=jax.ShapeDtypeStruct((ROWS, RANK...  47.5 us
    pallas_call x1, Pallas kernels, inverse_factor(): pl.pallas_call(inverse_kernel, out_shape=(shape, shape), in_specs=[VMEM],...  31.1 us
    pallas_call x1, Pallas kernels, gram_sum(): pl.pallas_call(gram_kernel, out_shape=jax.ShapeDtypeStruct((RANK, RANK),...  21.1 us
    pallas_call x1, Pallas kernels, row_sum(): pl.pallas_call(row_sum_kernel, out_shape=jax.ShapeDtypeStruct((COLS, RANK...  19 us
    dot_general x4, matrix products, contract_rows(): lax.dot_general(left, right, (((0,), (0,)), ((), ())), preferred_element_...  12.8 us
    pallas_call x1, Pallas kernels, row_scatter(): pl.pallas_call(row_scatter_kernel, out_shape=jax.ShapeDtypeStruct((COLS,...  9.13 us
    dot_general x3, matrix products, split_dot(): lax.dot_general(left, term, dims, preferred_element_type=F32)  4.39 us

profile of v1, /device:TPU:6, one launch (start us, length us, event | category | flops | bytes accessed | tf_op | source)
XLA Modules:
  0.0 205.9 jit_solution(4488198221511655233)
XLA Ops:
  0.6 0.0 copy-start
  0.6 1.4 fusion.20
  2.0 0.6 compare_convert_fusion
  2.7 0.7 compare_convert_fusion.1
  3.4 0.0 copy-start.3
  3.4 0.0 copy-start.4
  3.4 4.5 %multiply_reduce_fusion.1 = f32[8192]{0:T(1024)S(1)} fusion(bf16[2,256,8192]{2,1,0:T(8,128)(2,1)} %param.5, bf16[2,256,448]{1,2,0:T(8,128)(2,1)} %param.6, bf16[256]{0:T(256)(128)(2,1)S(1)} %compare_convert_fusion.1), kind=kOutput, calls=%fused_computation.1 | convolution fusion | flops 1886494720 | bytes 4456960 | tf_op jit(solution)/shard_map/dot_general | solution.py:552
  7.9 0.2 copy-done.3
  8.1 0.0 copy-done.4
  8.1 2.1 %multiply_reduce_fusion = f32[8192]{0:T(1024)S(1)} fusion(bf16[2,256,8192]{2,1,0:T(8,128)(2,1)S(1)} %copy-done.3, bf16[2,256,448]{1,2,0:T(8,128)(2,1)S(1)} %copy-done.4, bf16[256]{0:T(256)(128)(2,1)S(1)} %compare_convert_fusion), kind=kOutput, calls=%fused_computation | convolution fusion | flops 1886494720 | bytes 4456960 | tf_op jit(solution)/shard_map/dot_general | solution.py:552
  10.3 1.3 fusion.21.x_ref
  11.6 53.8 %first_sums.1 = (bf16[2048,512]{1,0:T(8,128)(2,1)S(1)}, f32[16,128]{1,0:T(8,128)S(1)}) custom-call(f32[2048,512]{1,0:T(8,128)S(1)} %fusion.21.x_ref, f32[64,128]{1,0:T(8,128)S(1)} %add_bitcast_fusion.f_ref), custom_call_target="tpu_custom_call" | custom-call | tf_op jit(solution)/shard_map/first_sums/pallas_call | solution.py:300
  65.4 1.1 fusion.4.x_ref
  66.5 19.0 %row_sum.1 = bf16[448,512]{1,0:T(8,128)(2,1)S(1)} custom-call(bf16[448,512]{1,0:T(8,128)(2,1)S(1)} %fusion.4.x_ref), custom_call_target="tpu_custom_call" | custom-call | tf_op jit(solution)/shard_map/row_sum/pallas_call | solution.py:374
  85.5 1.3 convolution_bitcast_fusion.x_ref
  86.9 47.5 %col_sum.1.y_ref = bf16[2048,512]{1,0:T(8,128)(2,1)S(1)} custom-call(f32[2048,512]{1,0:T(8,128)S(1)} %convolution_bitcast_fusion.x_ref, f32[16,128]{1,0:T(8,128)S(1)} %get-tuple-element.7.scale_ref), custom_call_target="tpu_custom_call" | custom-call | tf_op jit(solution)/shard_map/col_sum/pallas_call | solution.py:325
  134.4 21.1 %gram_sum.1.g_ref = f32[512,512]{1,0:T(8,128)S(1)} custom-call(bf16[2048,512]{1,0:T(8,128)(2,1)S(1)} %col_sum.1.y_ref), custom_call_target="tpu_custom_call" | custom-call | tf_op jit(solution)/shard_map/gram_sum/pallas_call | solution.py:417
  155.5 31.1 %inverse_factor.1 = (bf16[512,512]{1,0:T(8,128)(2,1)S(1)}, bf16[512,512]{1,0:T(8,128)(2,1)S(1)}) custom-call(f32[512,512]{1,0:T(8,128)S(1)} %gram_sum.1.g_ref), custom_call_target="tpu_custom_call" | custom-call | tf_op jit(solution)/shard_map/inverse_factor/pallas_call | solution.py:540
  186.6 0.2 fusion.16
  186.8 0.9 fusion.6
  187.8 3.2 %fusion.22 = f32[2048,512]{1,0:T(8,128)} fusion(bf16[2048,512]{1,0:T(8,128)(2,1)S(1)} %col_sum.1.y_ref, bf16[512,512]{1,0:T(8,128)(2,1)S(1)} %get-tuple-element.8), kind=kOutput, calls=%fused_computation.32 | convolution fusion | flops 1073741824 | bytes 6815744 | tf_op jit(solution)/shard_map/dot_general | solution.py:557
  191.0 5.1 %fusion.5.x_ref = bf16[448,512]{1,0:T(8,128)(2,1)S(1)} fusion(bf16[2048,448]{0,1:T(8,128)(2,1)S(1)} %copy-done, f32[2048,512]{1,0:T(8,128)} %fusion.22, bf16[2048,512]{1,0:T(8,128)(2,1)} %copy-done.1, bf16[512,512]{1,0:T(8,128)(2,1)S(1)} %get-tuple-element.9, f32[2048]{0:T(1024)S(1)} %bitcast.38), kind=kOutput, calls=%fused_computation.11 | convolution fusion | flops 2016641024 | bytes 9117696 | tf_op jit(solution)/shard_map/dot_general | solution.py:552
  196.0 9.1 %row_scatter.1 = f32[448,128]{1,0:T(8,128)S(1)} custom-call(bf16[448,512]{1,0:T(8,128)(2,1)S(1)} %fusion.5.x_ref), custom_call_target="tpu_custom_call" | custom-call | tf_op jit(solution)/shard_map/row_scatter/pallas_call | solution.py:459
  205.2 0.7 copy.10
  (6 shorter events, 0.0 us)
Async XLA Ops:
  0.6 9.6 %copy-start = (bf16[2048,448]{0,1:T(8,128)(2,1)S(1)}, bf16[2048,448]{0,1:T(8,128)(2,1)}, u32[]{:S(2)}) copy-start(bf16[2048,448]{0,1:T(8,128)(2,1)} %param.8) | copy-start | bytes 5505028
  3.4 4.8 %copy-start.3 = (bf16[2,256,8192]{2,1,0:T(8,128)(2,1)S(1)}, bf16[2,256,8192]{2,1,0:T(8,128)(2,1)}, u32[]{:S(2)}) copy-start(bf16[2,256,8192]{2,1,0:T(8,128)(2,1)} %param.5) | copy-start | bytes 25165828
  3.4 4.8 %copy-start.4 = (bf16[2,256,448]{1,2,0:T(8,128)(2,1)S(1)}, bf16[2,256,448]{1,2,0:T(8,128)(2,1)}, u32[]{:S(2)}) copy-start(bf16[2,256,448]{1,2,0:T(8,128)(2,1)} %param.6) | copy-start | bytes 1376260
  8.1 2.1 %copy-start.2 = (bf16[448,512]{1,0:T(8,128)(2,1)S(1)}, bf16[448,512]{1,0:T(8,128)(2,1)}, u32[]{:S(2)}) copy-start(bf16[448,512]{1,0:T(8,128)(2,1)} %param.9) | copy-start | bytes 1376260
  134.4 53.4 %copy-start.1 = (bf16[2048,512]{1,0:T(8,128)(2,1)}, bf16[2048,512]{1,0:T(8,128)(2,1)S(1)}, u32[]{:S(2)}) copy-start(bf16[2048,512]{1,0:T(8,128)(2,1)S(1)} %col_sum.1.y_ref) | copy-start | bytes 6291460

commit v2 on v1

--- a/solution.py
+++ b/solution.py
@@ -31,6 +31,11 @@
         self.send_sems, self.recv_sems, self.copies = send_sems, recv_sems, []
 
     def send(self, src, dst, device):
+        copy = self.make(src, dst, device)
+        copy.start()
+        return copy
+
+    def make(self, src, dst, device):
         slot = len(self.copies)
         copy = pltpu.make_async_remote_copy(
             src_ref=src,
@@ -40,7 +45,6 @@
             device_id=device,
             device_id_type=MESH,
         )
-        copy.start()
         self.copies.append(copy)
         return copy
 
@@ -379,91 +383,6 @@
         scratch_shapes=ring_scratch(10, 64, 48, RANK, BF16),
         compiler_params=params(2, 8),
         name="row_sum",
-    )(x)
-
-
-def gram_kernel(y_ref, o_ref, send_sems, recv_sems, got_f, got_b, sum_f, sum_b, own):
-    net = Net(send_sems, recv_sems)
-    row, col, core, z, y = place()
-    partner = (row, (y * 8 + z) * 2 + 1 - core)
-    ring, peers = row_ring(net, 64, 32)
-    half = core * 256
-    left = y_ref[:, pl.ds(pl.multiple_of(half, 128), 256)]
-    own[...] = lax.dot_general(left, y_ref[...], (((0,), (0,)), ((), ())), preferred_element_type=F32)
-    greet(peers + [partner])
-    src = functools.partial(at_rows, own, step=8)
-
-    def dst(start, count):
-        return at_rows(o_ref, half + start, count, 8)
-
-    ring.reduce_start(src, got_f, got_b)
-    ring.reduce_relay(src, got_f, got_b, sum_f, sum_b)
-    top, low = ring.reduce_end(src, got_f, got_b)
-    dst(ring.own, 32)[...] = top
-    dst(ring.own + 32, 32)[...] = low
-    ring.gather_start(dst)
-    swaps = [net.send(dst(ring.own, 64), dst(ring.own, 64), partner)]
-    ring.gather_relay(dst)
-    for start in (ring.last, ring.next):
-        swaps.append(net.send(dst(start, 64), dst(start, 64), partner))
-    ring.gather_end()
-    swaps.append(net.send(dst(ring.far, 64), dst(ring.far, 64), partner))
-    for copy in swaps:
-        copy.wait_recv()
-    net.drain()
-
-
-def gram_sum(y):
-    return pl.pallas_call(
-        gram_kernel,
-        out_shape=jax.ShapeDtypeStruct((RANK, RANK), F32),
-        in_specs=[VMEM],
-        out_specs=VMEM,
-        scratch_shapes=ring_scratch(14, 32, 32, RANK, F32) + [pltpu.VMEM((256, RANK), F32)],
-        compiler_params=params(3, 12),
-        name="gram_sum",
-    )(y)
-
-
-def row_scatter_kernel(x_ref, o_ref, send_sems, recv_sems, got_f, got_b, sum_f, sum_b):
-    net = Net(send_sems, recv_sems)
-    ring, peers = row_ring(net, 1, 1)
-    greet(peers)
-
-    def src(where, count):
-        return x_ref.at[pl.ds(where[1], count), pl.ds(pl.multiple_of(where[0] * 128, 128), 128)]
-
-    send = net.send
-    red = [
-        send(src((ring.far, 0), 224), got_f.at[0], ring.up),
-        send(src((ring.far, 224), 224), got_b.at[0], ring.down),
-        send(src((ring.next, 224), 224), got_b.at[1], ring.up),
-        send(src((ring.last, 0), 224), got_f.at[1], ring.down),
-    ]
-    red[0].wait_recv()
-    sum_f[...] = (f32(got_f.at[0]) + f32(src((ring.next, 0), 224))).astype(BF16)
-    red.append(send(sum_f, got_f.at[2], ring.up))
-    red[1].wait_recv()
-    sum_b[...] = (f32(got_b.at[0]) + f32(src((ring.last, 224), 224))).astype(BF16)
-    red.append(send(sum_b, got_b.at[2], ring.down))
-    for copy in red[2:]:
-        copy.wait_recv()
-    top = f32(src((ring.own, 0), 224)) + f32(got_f.at[1]) + f32(got_f.at[2])
-    low = f32(src((ring.own, 224), 224)) + f32(got_b.at[1]) + f32(got_b.at[2])
-    o_ref[pl.ds(0, 224)] = top * math.sqrt(FF)
-    o_ref[pl.ds(224, 224)] = low * math.sqrt(FF)
-    net.drain()
-
-
-def row_scatter(x):
-    return pl.pallas_call(
-        row_scatter_kernel,
-        out_shape=jax.ShapeDtypeStruct((COLS, RANK // 4), F32),
-        in_specs=[VMEM],
-        out_specs=VMEM,
-        scratch_shapes=ring_scratch(6, 224, 224, 128, BF16),
-        compiler_params=params(4, 8),
-        name="row_scatter",
     )(x)
 
 
@@ -510,56 +429,113 @@
     return jnp.concatenate(t, axis=0)
 
 
-def inverse_kernel(g_ref, high_ref, low_ref, x_ref):
+def dot(a, b, dims, precision=None):
+    return lax.dot_general(a, b, (dims, ((), ())), precision=precision, preferred_element_type=F32)
+
+
+def tail_kernel(
+    y_ref, scaled_ref, basis_ref, coef_ref, send_sems, recv_sems, got_f, got_b, sum_f, sum_b, own, g_ref, x_ref, m_ref, part, got, whole
+):
+    exact = lax.Precision.HIGHEST
+    net = Net(send_sems, recv_sems)
+    row, col, core, z, y = place()
+    partner = (row, (y * 8 + z) * 2 + 1 - core)
+    ring, peers = row_ring(net, 64, 32)
+    far = (lax.rem(row + 2, 4), col)
+    half = core * 256
+    left = y_ref[:, pl.ds(pl.multiple_of(half, 128), 256)]
+    own[...] = dot(left, y_ref[...], ((0,), (0,)))
+    greet(peers + [far, partner])
+    src = functools.partial(at_rows, own, step=8)
+
+    def dst(start, count):
+        return at_rows(g_ref, half + start, count, 8)
+
+    ring.reduce_start(src, got_f, got_b)
+    part[...] = dot(scaled_ref[...], y_ref[...], ((1,), (0,)))
+    ring.reduce_relay(src, got_f, got_b, sum_f, sum_b)
+    top, low = ring.reduce_end(src, got_f, got_b)
+    dst(ring.own, 32)[...] = top
+    dst(ring.own + 32, 32)[...] = low
+    ring.gather_start(dst)
+    swaps = [net.send(dst(ring.own, 64), dst(ring.own, 64), partner)]
+    ring.gather_relay(dst)
+    for start in (ring.last, ring.next):
+        swaps.append(net.send(dst(start, 64), dst(start, 64), partner))
+    ring.gather_end()
+    swaps.append(net.send(dst(ring.far, 64), dst(ring.far, 64), partner))
+
+    chunk = COLS // 4
+    xpeer = [peers[0], far, peers[1]]
+    for d in range(3):
+        net.send(at_rows(part, lax.rem(row + d + 1, 4) * chunk, chunk), got.at[d], xpeer[d])
+    scatter = net.copies[-3:]
+    mine, summed = at_rows(part, row * chunk, chunk), at_rows(whole, row * chunk, chunk)
+    gather = [net.make(summed, summed, peer) for peer in xpeer]
+    for copy in swaps:
+        copy.wait_recv()
+    x_ref[...] = g_ref[...]
+
     size = 128
-    x_ref[...] = g_ref[...]
     eye = lax.broadcasted_iota(jnp.int32, (size, size), 0) == lax.broadcasted_iota(jnp.int32, (size, size), 1)
-
-    def dot(a, b, dims):
-        return lax.dot_general(a, b, (dims, ((), ())), precision=lax.Precision.HIGHEST, preferred_element_type=F32)
 
     def block(k, carry):
         at = pl.ds(pl.multiple_of(k * size, size), size)
         unit = unit_inverse(x_ref[at, at])
         x_ref[:, at] = jnp.zeros((RANK, size), F32)
         x_ref[at, at] = eye.astype(F32)
-        line = dot(unit, x_ref[at, :], ((1,), (0,)))
+        line = dot(unit, x_ref[at, :], ((1,), (0,)), exact)
         later = lax.broadcasted_iota(jnp.int32, (size, RANK), 1) >= (k + 1) * size
-        done = jnp.where(later, 0.0, line)
-        high = done.astype(BF16)
-        high_ref[at, :] = high
-        low_ref[at, :] = (done - high.astype(F32)).astype(BF16)
-        x_ref[...] = x_ref[...] - dot(jnp.where(later, line, 0.0), line, ((0,), (0,)))
+        m_ref[at, :] = jnp.where(later, 0.0, line)
+        x_ref[...] = x_ref[...] - dot(jnp.where(later, line, 0.0), line, ((0,), (0,)), exact)
+
+        @pl.when(k == 1)
+        def _():
+            for copy in scatter:
+                copy.wait_recv()
+            summed[...] = mine[...] + got[0] + got[1] + got[2]
+            for copy in gather:
+                copy.start()
+
         return carry
 
     lax.fori_loop(0, RANK // size, block, 0)
-
-
-def inverse_factor(g):
-    shape = jax.ShapeDtypeStruct((RANK, RANK), BF16)
+    rows = y_ref[pl.ds(pl.multiple_of(col * 32, 16), 32)].astype(F32)
+    basis_ref[...] = dot(rows, m_ref[...], ((1,), (1,)), exact) * math.sqrt(DIM)
+    for copy in gather:
+        copy.wait_recv()
+    mine_rows = m_ref[pl.ds(pl.multiple_of(row * 128, 128), 128)]
+    coef_ref[...] = dot(whole[...], mine_rows, ((1,), (1,)), exact) * math.sqrt(FF)
+    net.drain()
+
+
+def outputs(second, scaled):
     return pl.pallas_call(
-        inverse_kernel,
-        out_shape=(shape, shape),
-        in_specs=[VMEM],
+        tail_kernel,
+        out_shape=(jax.ShapeDtypeStruct((32, RANK), F32), jax.ShapeDtypeStruct((COLS, RANK // 4), F32)),
+        in_specs=[VMEM, VMEM],
         out_specs=(VMEM, VMEM),
-        scratch_shapes=[pltpu.VMEM((RANK, RANK), F32)],
-        compiler_params=pltpu.CompilerParams(vmem_limit_bytes=16 << 20),
-        name="inverse_factor",
-    )(g)
+        scratch_shapes=ring_scratch(20, 32, 32, RANK, F32)
+        + [
+            pltpu.VMEM((256, RANK), F32),
+            pltpu.VMEM((RANK, RANK), F32),
+            pltpu.VMEM((RANK, RANK), F32),
+            pltpu.VMEM((RANK, RANK), F32),
+            pltpu.VMEM((COLS, RANK), F32),
+            pltpu.VMEM((3, COLS // 4, RANK), F32),
+            pltpu.VMEM((COLS, RANK), F32),
+        ],
+        compiler_params=params(3, 24),
+        name="outputs",
+    )(second, scaled)
 
 
 def contract_rows(left, right):
     return lax.dot_general(left, right, (((0,), (0,)), ((), ())), preferred_element_type=F32)
 
 
-def split_dot(left, right):
-    dims = (((1,), (1,)), ((), ()))
-    return sum(lax.dot_general(left, term, dims, preferred_element_type=F32) for term in right)
-
-
 def local(activations, out_grads, valid_len, weight, sketch):
     seq_dev, length, width = activations.shape
-    col_index = lax.axis_index("col")
     positions = lax.iota(jnp.int32, length)
     raw = jnp.dot(weight, sketch, preferred_element_type=F32)
     mass = jnp.zeros((width,), F32)
@@ -570,12 +546,9 @@
     weighted, scale = first_sums(raw, mass.reshape(64, 128))
     projected = row_sum(contract_rows(weight, weighted).astype(BF16))
     second = col_sum(jnp.dot(weight, projected, preferred_element_type=F32), scale)
-    scale = scale.reshape(ROWS, 1)
-    inverse = inverse_factor(gram_sum(second))
-    basis = split_dot(second, inverse)
-    own = split_dot(lax.dynamic_slice_in_dim(second, col_index * 32, 32, 0), inverse)
-    part = contract_rows(weight, (scale * basis).astype(BF16)).astype(BF16)
-    return own * math.sqrt(DIM), row_scatter(part).T
+    scaled = (weight.T.astype(F32) * scale.reshape(1, ROWS)).astype(BF16)
+    basis, coeffs = outputs(second, scaled)
+    return basis, coeffs.T
 
 
 def solution(mesh):

time: 207 us -> 194 us (0.937)
  matrix products: 19.8 us -> 10.4 us
  Pallas kernels: 182 us -> 177 us
    pallas_call x3 -> x1, Pallas kernels: 61.3 us -> 56 us  [outputs(): pl.pallas_call(tail_kernel, out_shape=(jax.ShapeDtypeStruct((32, RANK), F...]
    dot_general x4 -> x3, matrix products: 12.8 us -> 7.75 us  [contract_rows(): lax.dot_general(left, right, (((0,), (0,)), ((), ())), preferred_element_...]
    dot_general x3 -> x0, matrix products: 4.39 us -> none  [split_dot(): lax.dot_general(left, term, dims, preferred_element_type=F32)]
where the time goes in v2:
time: 194 us; the launch traced here: 192 us
  Pallas kernels  177 us (91%)
  matrix products  10.4 us (5%)
  local copies, waits for them, and re-layouts  2.66 us (1%)
    pallas_call x1, Pallas kernels, outputs(): pl.pallas_call(tail_kernel, out_shape=(jax.ShapeDtypeStruct((32, RANK), F...  56 us
    pallas_call x1, Pallas kernels, first_sums(): pl.pallas_call(first_kernel, out_shape=(jax.ShapeDtypeStruct((ROWS, RANK)...  53.8 us
    pallas_call x1, Pallas kernels, col_sum(): pl.pallas_call(col_sum_kernel, out_shape=jax.ShapeDtypeStruct((ROWS, RANK...  47.9 us
    pallas_call x1, Pallas kernels, row_sum(): pl.pallas_call(row_sum_kernel, out_shape=jax.ShapeDtypeStruct((COLS, RANK...  19 us
    dot_general x3, matrix products, contract_rows(): lax.dot_general(left, right, (((0,), (0,)), ((), ())), preferred_element_...  7.75 us

profile of v2, /device:TPU:6, one launch (start us, length us, event | category | flops | bytes accessed | tf_op | source)
XLA Modules:
  0.0 192.2 jit_solution(13875955596971642529)
XLA Ops:
  0.6 0.0 copy-start
  0.6 1.3 fusion.14
  2.0 0.6 compare_convert_fusion
  2.6 0.0 copy-start.2
  2.6 0.0 copy-start.3
  2.6 4.5 %multiply_reduce_fusion = f32[8192]{0:T(1024)S(1)} fusion(bf16[2,256,8192]{2,1,0:T(8,128)(2,1)} %param.5, bf16[2,256,448]{1,2,0:T(8,128)(2,1)} %param.6, bf16[256]{0:T(256)(128)(2,1)S(1)} %compare_convert_fusion), kind=kOutput, calls=%fused_computation | convolution fusion | flops 1886494720 | bytes 4456960 | tf_op jit(solution)/shard_map/dot_general | solution.py:534
  7.2 0.7 compare_convert_fusion.1
  7.8 0.0 copy-done.2
  7.9 0.0 copy-done.3
  7.9 0.0 copy-start.1
  7.9 2.1 %multiply_reduce_fusion.1 = f32[8192]{0:T(1024)S(1)} fusion(bf16[2,256,8192]{2,1,0:T(8,128)(2,1)S(1)} %copy-done.2, bf16[2,256,448]{1,2,0:T(8,128)(2,1)S(1)} %copy-done.3, bf16[256]{0:T(256)(128)(2,1)S(1)} %compare_convert_fusion.1), kind=kOutput, calls=%fused_computation.1 | convolution fusion | flops 1886494720 | bytes 4456960 | tf_op jit(solution)/shard_map/dot_general | solution.py:534
  10.0 0.0 copy-done
  10.0 0.0 copy-done.1
  10.0 1.3 fusion.15.x_ref
  11.3 53.8 %first_sums.1 = (bf16[2048,512]{1,0:T(8,128)(2,1)S(1)}, f32[16,128]{1,0:T(8,128)S(1)}) custom-call(f32[2048,512]{1,0:T(8,128)S(1)} %fusion.15.x_ref, f32[64,128]{1,0:T(8,128)S(1)} %add_bitcast_fusion.f_ref), custom_call_target="tpu_custom_call" | custom-call | tf_op jit(solution)/shard_map/first_sums/pallas_call | solution.py:304
  65.2 1.1 fusion.5.x_ref
  66.3 19.0 %row_sum.1 = bf16[448,512]{1,0:T(8,128)(2,1)S(1)} custom-call(bf16[448,512]{1,0:T(8,128)(2,1)S(1)} %fusion.5.x_ref), custom_call_target="tpu_custom_call" | custom-call | tf_op jit(solution)/shard_map/row_sum/pallas_call | solution.py:378
  85.3 1.3 convolution_bitcast_fusion.x_ref
  86.6 47.9 %col_sum.1.y_ref = bf16[2048,512]{1,0:T(8,128)(2,1)S(1)} custom-call(f32[2048,512]{1,0:T(8,128)S(1)} %convolution_bitcast_fusion.x_ref, f32[16,128]{1,0:T(8,128)S(1)} %get-tuple-element.7.scale_ref), custom_call_target="tpu_custom_call" | custom-call | tf_op jit(solution)/shard_map/col_sum/pallas_call | solution.py:329
  134.5 0.4 fusion.4.scaled_ref
  134.9 56.0 %outputs.1 = (f32[32,512]{1,0:T(8,128)S(1)}, f32[448,128]{1,0:T(8,128)S(1)}) custom-call(bf16[2048,512]{1,0:T(8,128)(2,1)S(1)} %col_sum.1.y_ref, bf16[448,2048]{1,0:T(8,128)(2,1)S(1)} %fusion.4.scaled_ref), custom_call_target="tpu_custom_call" | custom-call | tf_op jit(solution)/shard_map/outputs/pallas_call | solution.py:513
  190.9 0.6 copy.11
  191.5 0.7 copy.12
  (1 shorter events, 0.0 us)
Async XLA Ops:
  0.6 9.4 %copy-start = (bf16[448,512]{1,0:T(8,128)(2,1)S(1)}, bf16[448,512]{1,0:T(8,128)(2,1)}, u32[]{:S(2)}) copy-start(bf16[448,512]{1,0:T(8,128)(2,1)} %param.9) | copy-start | bytes 1376260
  2.6 5.2 %copy-start.2 = (bf16[2,256,8192]{2,1,0:T(8,128)(2,1)S(1)}, bf16[2,256,8192]{2,1,0:T(8,128)(2,1)}, u32[]{:S(2)}) copy-start(bf16[2,256,8192]{2,1,0:T(8,128)(2,1)} %param.5) | copy-start | bytes 25165828
  2.6 5.2 %copy-start.3 = (bf16[2,256,448]{1,2,0:T(8,128)(2,1)S(1)}, bf16[2,256,448]{1,2,0:T(8,128)(2,1)}, u32[]{:S(2)}) copy-start(bf16[2,256,448]{1,2,0:T(8,128)(2,1)} %param.6) | copy-start | bytes 1376260
  7.9 2.1 %copy-start.1 = (bf16[2048,448]{0,1:T(8,128)(2,1)S(1)}, bf16[2048,448]{0,1:T(8,128)(2,1)}, u32[]{:S(2)}) copy-start(bf16[2048,448]{0,1:T(8,128)(2,1)} %param.8) | copy-start | bytes 5505028

commit v3 on v2

--- a/solution.py
+++ b/solution.py
@@ -115,7 +115,7 @@
         self.gat[3].wait_recv()
 
 
-def col_sum_steps(net, x_ref, o_ref, scale_ref, square, pair, mine, got_f, got_b, sum_f, sum_b, ysum, zgot):
+def col_sum_steps(net, x_ref, o_ref, rescale, pair, mine, got_f, got_b, sum_f, sum_b, ysum, zgot):
     row, _, core, z, y = place()
 
     def at(yy, zz, kk):
@@ -135,15 +135,6 @@
 
     def src(p):
         return lambda start, count: mine.at[p, pl.ds(pl.multiple_of(start, 16), count)]
-
-    def own_scale():
-        start = base + y * YCH + z * ZCH
-        line = scale_ref[pl.ds(start // 128, 1), :]
-        lanes = lax.broadcasted_iota(jnp.int32, (ZCH, 128), 1)
-        rows = lax.broadcasted_iota(jnp.int32, (ZCH, 128), 0)
-        picked = jnp.where(lanes == rows + lax.rem(start, 128), line, 0.0)
-        scale = jnp.sum(picked, axis=1, keepdims=True)
-        return scale * scale if square else scale
 
     def s0(p):
         half = x_ref.at[pl.ds(pl.multiple_of(other, 16), HALF), cols(p)]
@@ -175,7 +166,7 @@
             state[p]["z"][d].wait_recv()
             total = total + f32(zgot.at[p, d])
         part = out(p, y * YCH + z * ZCH, ZCH)
-        part[...] = (total * own_scale()).astype(BF16)
+        part[...] = rescale(total, base + y * YCH + z * ZCH).astype(BF16)
         state[p]["g"] = [net.send(part, part, peer) for peer in zpeer]
 
     def s5(p):
@@ -206,7 +197,6 @@
     return [s0, s1, s2, s3, s4, s5, s6, s7, s8], [partner, up, down] + zpeer
 
 
-COL_COPIES = PIECES * 29
 COL_SCRATCH = [
     pltpu.VMEM((PIECES, HALF, WIDE), F32),
     pltpu.VMEM((PIECES, HALF, WIDE), BF16),
@@ -219,8 +209,10 @@
 ]
 
 
-ORDER = (0.0, 2.5, 5.0, 7.5, 14.0, 19.0, 22.0, 24.5, 26.0)
-GAPS = (0.1, 1.8, 2.2, 2.2, 4.0, 4.0, 4.0, 4.0, 4.0)
+LINK = (0.0, 2.5, 5.0, 7.5, 14.0, 19.0, 22.0, 24.5, 26.0)
+TURN = (26.2, 28.8, 31.0, 33.5, 36.0)
+ORDER = LINK + TURN + tuple(36.5 + t for t in LINK)
+GAPS = (0.1, 1.8, 2.2, 2.2) + (4.5,) * 19
 
 
 def run_steps(steps, extra=()):
@@ -233,20 +225,8 @@
             steps[s](n)
 
 
-def col_sum_kernel(x_ref, scale_ref, o_ref, send_sems, recv_sems, *scratch):
-    net = Net(send_sems, recv_sems)
-    steps, peers = col_sum_steps(net, x_ref, o_ref, scale_ref, False, *scratch)
-    greet(peers)
-    run_steps(steps)
-    net.drain()
-
-
-def first_kernel(x_ref, f_ref, o_ref, scale_ref, send_sems, recv_sems, fx, f1, fc, f2, fy, f3, fz, ft, fg, *scratch):
-    net = Net(send_sems, recv_sems)
-    steps, peers = col_sum_steps(net, x_ref, o_ref, scale_ref, True, *scratch)
-    row, col, core, z, y = place()
-    xpeer = [(lax.rem(row + d, 4), col) for d in range(1, 4)]
-    far = (row, (lax.rem(y + 2, 4) * 8 + z) * 2 + core)
+def fisher_steps(net, f_ref, scale_ref, peers, far, xpeer, fx, f1, fc, f2, fy, f3, fz, ft, fg):
+    row = lax.axis_index("row")
     ypeer = [peers[1], far, peers[2]]
     state = {}
 
@@ -288,8 +268,70 @@
         mass = jnp.sum(ft[...] + fg[0] + fg[1] + fg[2], keepdims=True)
         scale_ref[...] = jnp.sqrt(scale_ref[...] / (mass / DIM + 1e-06))
 
+    return [t0, t1, t2, t3, t4, t5]
+
+
+def chain_kernel(
+    x_ref, f_ref, weight_ref, y_ref, scaled_ref, send_sems, recv_sems, scale_ref, first, back, again, part, xgot_f, xgot_b,
+    xsum_f, xsum_b, projected, *scratch
+):
+    net = Net(send_sems, recv_sems)
+    row, col, core, z, y = place()
+
+    def rescale(total, start):
+        line = scale_ref[pl.ds(start // 128, 1), :]
+        lanes = lax.broadcasted_iota(jnp.int32, (ZCH, 128), 1)
+        rows = lax.broadcasted_iota(jnp.int32, (ZCH, 128), 0)
+        picked = jnp.where(lanes == rows + lax.rem(start, 128), line, 0.0)
+        return total * jnp.sum(picked, axis=1, keepdims=True)
+
+    sum1, peers = col_sum_steps(net, x_ref, first, rescale, *scratch[:8])
+    sum2, _ = col_sum_steps(net, again, y_ref, lambda total, start: total, *scratch[8:16])
+    xpeer = [(lax.rem(row + d, 4), col) for d in range(1, 4)]
+    far = (row, (lax.rem(y + 2, 4) * 8 + z) * 2 + core)
+    fisher = fisher_steps(net, f_ref, scale_ref, peers, far, xpeer, *scratch[16:])
+    rings = [Ring(net, row, xpeer[0], xpeer[2], COLS // 4, 64) for _ in range(PIECES)]
+
+    def scale_weight(n):
+        def step():
+            for b in range(4 * n, 4 * n + 4):
+                at = pl.ds(b * 128, 128)
+                block = weight_ref[:, at].astype(F32) * scale_ref[b : b + 1, :]
+                scaled_ref[:, at] = block.astype(BF16)
+                back[at, :] = block.T.astype(BF16)
+
+        return step
+
+    def src(p):
+        return lambda start, count: at_rows(part.at[p], start, count)
+
+    def dst(p):
+        return lambda start, count: at_rows(projected.at[p], start, count)
+
+    def q0(p):
+        part[p] = dot(scaled_ref[...], first[:, pl.ds(p * WIDE, WIDE)], ((1,), (0,))).astype(BF16)
+        rings[p].reduce_start(src(p), xgot_f.at[p], xgot_b.at[p])
+
+    def q1(p):
+        rings[p].reduce_relay(src(p), xgot_f.at[p], xgot_b.at[p], xsum_f.at[p], xsum_b.at[p])
+
+    def q2(p):
+        top, low = rings[p].reduce_end(src(p), xgot_f.at[p], xgot_b.at[p])
+        dst(p)(rings[p].own, 64)[...] = top.astype(BF16)
+        dst(p)(rings[p].own + 64, 48)[...] = low.astype(BF16)
+        rings[p].gather_start(dst(p))
+
+    def q3(p):
+        rings[p].gather_relay(dst(p))
+
+    def q4(p):
+        rings[p].gather_end()
+        again[:, pl.ds(p * WIDE, WIDE)] = dot(back[...], projected[p], ((1,), (0,)))
+
     greet(peers + [far] + xpeer)
-    run_steps(steps, ((-1.0, t0), (2.6, t1), (3.9, t2), (7.0, t3), (11.5, t4), (13.9, t5)))
+    extra = list(zip((-1.0, 2.6, 3.9, 7.0, 11.5, 13.9), fisher))
+    extra += [(when, scale_weight(n)) for n, when in enumerate((14.5, 18.0, 20.0, 23.0))]
+    run_steps(sum1 + [q0, q1, q2, q3, q4] + sum2, extra)
     net.drain()
 
 
@@ -299,16 +341,31 @@
     )
 
 
-def first_sums(raw, mass):
+def chain(raw, mass, weight):
     piece = (16, 128)
+    copies = PIECES * 68 + 17
     return pl.pallas_call(
-        first_kernel,
-        out_shape=(jax.ShapeDtypeStruct((ROWS, RANK), BF16), jax.ShapeDtypeStruct(piece, F32)),
-        in_specs=[VMEM, VMEM],
+        chain_kernel,
+        out_shape=(jax.ShapeDtypeStruct((ROWS, RANK), BF16), jax.ShapeDtypeStruct((COLS, ROWS), BF16)),
+        in_specs=[VMEM, VMEM, VMEM],
         out_specs=(VMEM, VMEM),
         scratch_shapes=[
-            pltpu.SemaphoreType.DMA((COL_COPIES + 17,)),
-            pltpu.SemaphoreType.DMA((COL_COPIES + 17,)),
+            pltpu.SemaphoreType.DMA((copies,)),
+            pltpu.SemaphoreType.DMA((copies,)),
+            pltpu.VMEM(piece, F32),
+            pltpu.VMEM((ROWS, RANK), BF16),
+            pltpu.VMEM((ROWS, COLS), BF16),
+            pltpu.VMEM((ROWS, RANK), F32),
+            pltpu.VMEM((PIECES, COLS, WIDE), BF16),
+            pltpu.VMEM((PIECES, 3, 64, WIDE), BF16),
+            pltpu.VMEM((PIECES, 3, 48, WIDE), BF16),
+            pltpu.VMEM((PIECES, 64, WIDE), BF16),
+            pltpu.VMEM((PIECES, 48, WIDE), BF16),
+            pltpu.VMEM((PIECES, COLS, WIDE), BF16),
+        ]
+        + COL_SCRATCH
+        + COL_SCRATCH
+        + [
             pltpu.VMEM((3,) + piece, F32),
             pltpu.VMEM(piece, F32),
             pltpu.VMEM(piece, F32),
@@ -318,27 +375,10 @@
             pltpu.VMEM((7,) + piece, F32),
             pltpu.VMEM((8, 128), F32),
             pltpu.VMEM((3, 8, 128), F32),
-        ]
-        + COL_SCRATCH,
-        compiler_params=params(0, 28),
-        name="first_sums",
-    )(raw, mass)
-
-
-def col_sum(x, scale):
-    return pl.pallas_call(
-        col_sum_kernel,
-        out_shape=jax.ShapeDtypeStruct((ROWS, RANK), BF16),
-        in_specs=[VMEM, VMEM],
-        out_specs=VMEM,
-        scratch_shapes=[
-            pltpu.SemaphoreType.DMA((COL_COPIES,)),
-            pltpu.SemaphoreType.DMA((COL_COPIES,)),
-        ]
-        + COL_SCRATCH,
-        compiler_params=params(1, 28),
-        name="col_sum",
-    )(x, scale)
+        ],
+        compiler_params=params(0, 44),
+        name="chain",
+    )(raw, mass, weight)
 
 
 def ring_scratch(copies, front, back, width, dtype):
@@ -356,34 +396,6 @@
     row, col, _, _, _ = place()
     up, down = (lax.rem(row + 1, 4), col), (lax.rem(row + 3, 4), col)
     return Ring(net, row, up, down, chunk, front), [up, down]
-
-
-def row_sum_kernel(x_ref, o_ref, send_sems, recv_sems, got_f, got_b, sum_f, sum_b):
-    net = Net(send_sems, recv_sems)
-    ring, peers = row_ring(net, 112, 64)
-    greet(peers)
-    src, dst = functools.partial(at_rows, x_ref), functools.partial(at_rows, o_ref)
-    ring.reduce_start(src, got_f, got_b)
-    ring.reduce_relay(src, got_f, got_b, sum_f, sum_b)
-    top, low = ring.reduce_end(src, got_f, got_b)
-    dst(ring.own, 64)[...] = top.astype(BF16)
-    dst(ring.own + 64, 48)[...] = low.astype(BF16)
-    ring.gather_start(dst)
-    ring.gather_relay(dst)
-    ring.gather_end()
-    net.drain()
-
-
-def row_sum(x):
-    return pl.pallas_call(
-        row_sum_kernel,
-        out_shape=jax.ShapeDtypeStruct((COLS, RANK), BF16),
-        in_specs=[VMEM],
-        out_specs=VMEM,
-        scratch_shapes=ring_scratch(10, 64, 48, RANK, BF16),
-        compiler_params=params(2, 8),
-        name="row_sum",
-    )(x)
 
 
 def unit_inverse(block):
@@ -543,10 +555,7 @@
         valid = (positions < valid_len[seq]).astype(BF16)
         grad = contract_rows(activations[seq], out_grads[seq] * valid[:, None])
         mass = mass + jnp.sum(grad * grad, axis=1)
-    weighted, scale = first_sums(raw, mass.reshape(64, 128))
-    projected = row_sum(contract_rows(weight, weighted).astype(BF16))
-    second = col_sum(jnp.dot(weight, projected, preferred_element_type=F32), scale)
-    scaled = (weight.T.astype(F32) * scale.reshape(1, ROWS)).astype(BF16)
+    second, scaled = chain(raw, mass.reshape(64, 128), weight.T)
     basis, coeffs = outputs(second, scaled)
     return basis, coeffs.T
 

time: 194 us -> 176 us (0.907)
  Pallas kernels: 177 us -> 161 us
  matrix products: 10.4 us -> 7.94 us
    pallas_call x3 -> x1, Pallas kernels: 121 us -> 105 us  [chain(): pl.pallas_call(chain_kernel, out_shape=(jax.ShapeDtypeStruct((ROWS, RANK)...]
    dot_general x3 -> x2, matrix products: 7.75 us -> 6.64 us  [contract_rows(): lax.dot_general(left, right, (((0,), (0,)), ((), ())), preferred_element_...]
where the time goes in v3:
time: 176 us; the launch traced here: 174 us
  Pallas kernels  161 us (91%)
  matrix products  7.94 us (5%)
  local copies, waits for them, and re-layouts  2.86 us (2%)
    pallas_call x1, Pallas kernels, chain(): pl.pallas_call(chain_kernel, out_shape=(jax.ShapeDtypeStruct((ROWS, RANK)...  105 us
    pallas_call x1, Pallas kernels, outputs(): pl.pallas_call(tail_kernel, out_shape=(jax.ShapeDtypeStruct((32, RANK), F...  55.9 us
    dot_general x2, matrix products, contract_rows(): lax.dot_general(left, right, (((0,), (0,)), ((), ())), preferred_element_...  6.64 us

profile of v3, /device:TPU:6, one launch (start us, length us, event | category | flops | bytes accessed | tf_op | source)
XLA Modules:
  0.0 174.2 jit_solution(8642296908409817937)
XLA Ops:
  0.6 0.0 copy-start
  0.6 1.3 fusion.12
  2.0 0.6 compare_convert_fusion
  2.6 0.7 compare_convert_fusion.1
  3.3 0.0 copy-start.2
  3.3 0.0 copy-start.3
  3.3 4.5 %multiply_reduce_fusion.1 = f32[8192]{0:T(1024)S(1)} fusion(bf16[2,256,8192]{2,1,0:T(8,128)(2,1)} %param.5, bf16[2,256,448]{1,2,0:T(8,128)(2,1)} %param.6, bf16[256]{0:T(256)(128)(2,1)S(1)} %compare_convert_fusion.1), kind=kOutput, calls=%fused_computation.1 | convolution fusion | flops 1886494720 | bytes 4456960 | tf_op jit(solution)/shard_map/dot_general | solution.py:546
  7.8 0.2 copy-done.2
  8.0 0.0 copy-done.3
  8.1 0.0 copy-start.1
  8.1 2.1 %multiply_reduce_fusion = f32[8192]{0:T(1024)S(1)} fusion(bf16[2,256,8192]{2,1,0:T(8,128)(2,1)S(1)} %copy-done.2, bf16[2,256,448]{1,2,0:T(8,128)(2,1)S(1)} %copy-done.3, bf16[256]{0:T(256)(128)(2,1)S(1)} %compare_convert_fusion), kind=kOutput, calls=%fused_computation | convolution fusion | flops 1886494720 | bytes 4456960 | tf_op jit(solution)/shard_map/dot_general | solution.py:546
  10.2 0.0 copy-done
  10.2 0.0 copy-done.1
  10.2 1.3 fusion.13.x_ref
  11.5 105.4 %chain.1 = (bf16[2048,512]{1,0:T(8,128)(2,1)S(1)}, bf16[448,2048]{1,0:T(8,128)(2,1)S(1)}) custom-call(f32[2048,512]{1,0:T(8,128)S(1)} %fusion.13.x_ref, f32[64,128]{1,0:T(8,128)S(1)} %add_bitcast_fusion.f_ref, bf16[448,2048]{1,0:T(8,128)(2,1)S(1)} %bitcast.20), custom_call_target="tpu_custom_call" | custom-call | tf_op jit(solution)/shard_map/chain/pallas_call | solution.py:347
  116.9 55.9 %outputs.1 = (f32[32,512]{1,0:T(8,128)S(1)}, f32[448,128]{1,0:T(8,128)S(1)}) custom-call(bf16[2048,512]{1,0:T(8,128)(2,1)S(1)} %get-tuple-element.6.y_ref, bf16[448,2048]{1,0:T(8,128)(2,1)S(1)} %get-tuple-element.7.scaled_ref), custom_call_target="tpu_custom_call" | custom-call | tf_op jit(solution)/shard_map/outputs/pallas_call | solution.py:525
  172.8 0.6 copy.9
  173.5 0.7 copy.10
  (1 shorter events, 0.0 us)
Async XLA Ops:
  0.6 9.5 %copy-start = (bf16[448,512]{1,0:T(8,128)(2,1)S(1)}, bf16[448,512]{1,0:T(8,128)(2,1)}, u32[]{:S(2)}) copy-start(bf16[448,512]{1,0:T(8,128)(2,1)} %param.9) | copy-start | bytes 1376260
  3.3 4.8 %copy-start.2 = (bf16[2,256,8192]{2,1,0:T(8,128)(2,1)S(1)}, bf16[2,256,8192]{2,1,0:T(8,128)(2,1)}, u32[]{:S(2)}) copy-start(bf16[2,256,8192]{2,1,0:T(8,128)(2,1)} %param.5) | copy-start | bytes 25165828
  3.3 4.8 %copy-start.3 = (bf16[2,256,448]{1,2,0:T(8,128)(2,1)S(1)}, bf16[2,256,448]{1,2,0:T(8,128)(2,1)}, u32[]{:S(2)}) copy-start(bf16[2,256,448]{1,2,0:T(8,128)(2,1)} %param.6) | copy-start | bytes 1376260
  8.1 2.1 %copy-start.1 = (bf16[2048,448]{0,1:T(8,128)(2,1)S(1)}, bf16[2048,448]{0,1:T(8,128)(2,1)}, u32[]{:S(2)}) copy-start(bf16[2048,448]{0,1:T(8,128)(2,1)} %param.8) | copy-start | bytes 5505028

commit v4 on v3

--- a/solution.py
+++ b/solution.py
@@ -12,10 +12,10 @@
 VMEM = pl.BlockSpec(memory_space=pltpu.VMEM)
 F32, BF16 = jnp.float32, jnp.bfloat16
 ROWS, COLS, RANK, DIM, FF = 2048, 448, 512, 8192, 28672
-HALF, YCH, ZCH = 1024, 256, 32
+HALF, YCH, ZCH, LEN = 1024, 256, 32, 256
 PIECES = 4
 WIDE = RANK // PIECES
-ZTYPE = F32
+ZTYPE = BF16
 
 
 def f32(ref):
@@ -57,7 +57,7 @@
     barrier = pltpu.get_barrier_semaphore()
     for peer in peers:
         pl.semaphore_signal(barrier, inc=1, device_id=peer, device_id_type=MESH)
-    pl.semaphore_wait(barrier, len(peers))
+    return lambda: pl.semaphore_wait(barrier, len(peers))
 
 
 def place():
@@ -209,20 +209,25 @@
 ]
 
 
-LINK = (0.0, 2.5, 5.0, 7.5, 14.0, 19.0, 22.0, 24.5, 26.0)
-TURN = (26.2, 28.8, 31.0, 33.5, 36.0)
-ORDER = LINK + TURN + tuple(36.5 + t for t in LINK)
-GAPS = (0.1, 1.8, 2.2, 2.2) + (4.5,) * 19
-
-
-def run_steps(steps, extra=()):
-    events = [(ORDER[s] + GAPS[s] * p, s, p) for s in range(len(steps)) for p in range(PIECES)]
-    events += [(when, -1, n) for n, (when, _) in enumerate(extra)]
-    for _, s, n in sorted(events):
-        if s < 0:
-            extra[n][1]()
+ORDER = (
+    100, 4, 5, 101, 102, 8, 9, 6, 103, 7, 12, 13, 10, 14, 11, 104,
+    105, 16, 17, 15, 110, 111, 112, 113, 18, 20, 21, 24, 19, 25, 22, 28,
+    32, 36, 29, 26, 33, 37, 23, 40, 30, 44, 41, 27, 34, 38, 48, 31,
+    45, 42, 35, 39, 52, 56, 46, 49, 43, 60, 50, 53, 57, 47, 64, 54,
+    58, 61, 51, 68, 62, 65, 55, 59, 66, 63, 69, 70, 72, 67, 71, 73,
+    74, 76, 75, 77, 78, 81, 80, 79, 82, 84, 83, 86, 85, 89, 90, 88,
+    87, 91,
+)
+
+
+def run_steps(steps, fisher, weight):
+    for event in ORDER:
+        if event >= 110:
+            weight[event - 110]()
+        elif event >= 100:
+            fisher[event - 100]()
         else:
-            steps[s](n)
+            steps[event // PIECES](event % PIECES)
 
 
 def fisher_steps(net, f_ref, scale_ref, peers, far, xpeer, fx, f1, fc, f2, fy, f3, fz, ft, fg):
@@ -266,13 +271,13 @@
         for copy in state["t"]:
             copy.wait_recv()
         mass = jnp.sum(ft[...] + fg[0] + fg[1] + fg[2], keepdims=True)
-        scale_ref[...] = jnp.sqrt(scale_ref[...] / (mass / DIM + 1e-06))
+        scale_ref[...] = jnp.sqrt(jnp.maximum(scale_ref[...], 0.0) / (mass / DIM + 1e-06))
 
     return [t0, t1, t2, t3, t4, t5]
 
 
 def chain_kernel(
-    x_ref, f_ref, weight_ref, y_ref, scaled_ref, send_sems, recv_sems, scale_ref, first, back, again, part, xgot_f, xgot_b,
+    sketch_ref, acts_ref, grads_ref, len_ref, weight_ref, y_ref, scaled_ref, send_sems, recv_sems, load_sems, x_ref, acts, f_ref, scale_ref, first, back, again, part, xgot_f, xgot_b,
     xsum_f, xsum_b, projected, *scratch
 ):
     net = Net(send_sems, recv_sems)
@@ -328,10 +333,36 @@
         rings[p].gather_end()
         again[:, pl.ds(p * WIDE, WIDE)] = dot(back[...], projected[p], ((1,), (0,)))
 
-    greet(peers + [far] + xpeer)
-    extra = list(zip((-1.0, 2.6, 3.9, 7.0, 11.5, 13.9), fisher))
-    extra += [(when, scale_weight(n)) for n, when in enumerate((14.5, 18.0, 20.0, 23.0))]
-    run_steps(sum1 + [q0, q1, q2, q3, q4] + sum2, extra)
+    arrived = greet(peers + [far] + xpeer)
+    loads = [pltpu.make_async_copy(acts_ref.at[n], acts.at[n], load_sems.at[n]) for n in range(2)]
+    for load in loads:
+        load.start()
+    for n in range(4):
+        at = pl.ds(n * 512, 512)
+        x_ref[at, :] = dot(weight_ref[:, at], sketch_ref[...], ((0,), (0,)))
+
+    def masses(n):
+        loads[n].wait()
+        valid = lax.broadcasted_iota(jnp.int32, (COLS, LEN), 1) < len_ref[n]
+        grads = jnp.where(valid, grads_ref[n].astype(F32), 0.0).astype(BF16)
+        tokens = dot(grads, grads, ((0,), (0,)))
+        high = tokens.astype(BF16)
+        low = (tokens - high.astype(F32)).astype(BF16)
+        for c in range(8):
+            block = acts[n, :, pl.ds(c * 1024, 1024)]
+            mixed = dot(high, block, ((1,), (0,))) + dot(low, block, ((1,), (0,)))
+            sums = jnp.sum(block.astype(F32) * mixed, axis=0, keepdims=True)
+            for i in range(8):
+                at = pl.ds(8 * c + i, 1)
+                line = sums[:, i * 128 : (i + 1) * 128]
+                f_ref[at, :] = line if n == 0 else f_ref[at, :] + line
+
+    masses(0)
+    arrived()
+    for p in range(PIECES):
+        sum1[0](p)
+    masses(1)
+    run_steps(sum1 + [q0, q1, q2, q3, q4] + sum2, fisher, [scale_weight(n) for n in range(4)])
     net.drain()
 
 
@@ -341,17 +372,27 @@
     )
 
 
-def chain(raw, mass, weight):
+def chain(sketch, acts, grads, lens, weight):
     piece = (16, 128)
     copies = PIECES * 68 + 17
     return pl.pallas_call(
         chain_kernel,
         out_shape=(jax.ShapeDtypeStruct((ROWS, RANK), BF16), jax.ShapeDtypeStruct((COLS, ROWS), BF16)),
-        in_specs=[VMEM, VMEM, VMEM],
+        in_specs=[
+            VMEM,
+            pl.BlockSpec(memory_space=pltpu.HBM),
+            VMEM,
+            pl.BlockSpec(memory_space=pltpu.SMEM),
+            VMEM,
+        ],
         out_specs=(VMEM, VMEM),
         scratch_shapes=[
             pltpu.SemaphoreType.DMA((copies,)),
             pltpu.SemaphoreType.DMA((copies,)),
+            pltpu.SemaphoreType.DMA((2,)),
+            pltpu.VMEM((ROWS, RANK), F32),
+            pltpu.VMEM((2, LEN, DIM), BF16),
+            pltpu.VMEM((64, 128), F32),
             pltpu.VMEM(piece, F32),
             pltpu.VMEM((ROWS, RANK), BF16),
             pltpu.VMEM((ROWS, COLS), BF16),
@@ -376,9 +417,9 @@
             pltpu.VMEM((8, 128), F32),
             pltpu.VMEM((3, 8, 128), F32),
         ],
-        compiler_params=params(0, 44),
+        compiler_params=params(0, 36),
         name="chain",
-    )(raw, mass, weight)
+    )(sketch, acts, grads, lens, weight)
 
 
 def ring_scratch(copies, front, back, width, dtype):
@@ -456,8 +497,9 @@
     far = (lax.rem(row + 2, 4), col)
     half = core * 256
     left = y_ref[:, pl.ds(pl.multiple_of(half, 128), 256)]
+    arrived = greet(peers + [far, partner])
     own[...] = dot(left, y_ref[...], ((0,), (0,)))
-    greet(peers + [far, partner])
+    arrived()
     src = functools.partial(at_rows, own, step=8)
 
     def dst(start, count):
@@ -542,20 +584,8 @@
     )(second, scaled)
 
 
-def contract_rows(left, right):
-    return lax.dot_general(left, right, (((0,), (0,)), ((), ())), preferred_element_type=F32)
-
-
 def local(activations, out_grads, valid_len, weight, sketch):
-    seq_dev, length, width = activations.shape
-    positions = lax.iota(jnp.int32, length)
-    raw = jnp.dot(weight, sketch, preferred_element_type=F32)
-    mass = jnp.zeros((width,), F32)
-    for seq in range(seq_dev):
-        valid = (positions < valid_len[seq]).astype(BF16)
-        grad = contract_rows(activations[seq], out_grads[seq] * valid[:, None])
-        mass = mass + jnp.sum(grad * grad, axis=1)
-    second, scaled = chain(raw, mass.reshape(64, 128), weight.T)
+    second, scaled = chain(sketch, activations, out_grads.transpose(0, 2, 1), valid_len, weight.T)
     basis, coeffs = outputs(second, scaled)
     return basis, coeffs.T
 

time: 176 us -> 171 us (0.972)
  matrix products: 7.94 us -> 0 us
  local copies, waits for them, and re-layouts: 2.86 us -> 8.88 us
  Pallas kernels: 161 us -> 159 us
    dot_general x3 -> x0, matrix products: 7.94 us -> none  [the longest x2 6.64 us: contract_rows(): lax.dot_general(left, right, (((0,), (0,)), ((), ())), preferred_element_...]
    unnamed x10 -> x12, local copies, waits for them, and re-layouts: 1.54 us -> 8.88 us
where the time goes in v4:
time: 171 us; the launch traced here: 169 us
  Pallas kernels  159 us (93%)
  local copies, waits for them, and re-layouts  8.88 us (5%)
    pallas_call x1, Pallas kernels, chain(): pl.pallas_call(chain_kernel, out_shape=(jax.ShapeDtypeStruct((ROWS, RANK)...  104 us
    pallas_call x1, Pallas kernels, outputs(): pl.pallas_call(tail_kernel, out_shape=(jax.ShapeDtypeStruct((32, RANK), F...  55.4 us
    unnamed x12, local copies, waits for them, and re-layouts  8.88 us

profile of v4, /device:TPU:6, one launch (start us, length us, event | category | flops | bytes accessed | tf_op | source)
XLA Modules:
  0.0 168.8 jit_solution(541360677708569320)
XLA Ops:
  0.6 0.0 copy-start
  0.6 3.4 %copy-done = bf16[2,256,8192]{2,1,0:T(8,128)(2,1)S(1)} copy-done((bf16[2,256,8192]{2,1,0:T(8,128)(2,1)S(1)}, bf16[2,256,8192]{2,1,0:T(8,128)(2,1)}, u32[]{:S(2)}) %copy-start) | copy-done | bytes 8388632
  4.0 0.0 copy-start.1
  4.0 1.5 copy-done.1
  5.5 0.0 copy-start.2
  5.5 1.0 copy-done.2
  6.5 0.0 copy-start.3
  6.5 1.0 copy-done.3
  7.6 0.0 copy-start.4
  7.6 0.7 copy-done.4
  8.2 103.8 %chain.1 = (bf16[2048,512]{1,0:T(8,128)(2,1)S(1)}, bf16[448,2048]{1,0:T(8,128)(2,1)S(1)}) custom-call(bf16[448,512]{1,0:T(8,128)(2,1)S(1)} %copy-done.2, bf16[2,256,8192]{2,1,0:T(8,128)(2,1)S(1)} %copy-done, bf16[2,448,256]{2,1,0:T(8,128)(2,1)S(1)} %bitcast.4, s32[2]{0:T(128)S(1)} %copy-done.4, bf16[448,2048]{1,0:T(8,128)(2,1)S(1)} %bitcast.3), custom_call_target="tpu_custom_call" | custom-call | tf_op jit(solution)/shard_map/chain/pallas_call | solution.py:378
  112.1 55.4 %outputs.1 = (f32[32,512]{1,0:T(8,128)S(1)}, f32[448,128]{1,0:T(8,128)S(1)}) custom-call(bf16[2048,512]{1,0:T(8,128)(2,1)S(1)} %get-tuple-element.6.y_ref, bf16[448,2048]{1,0:T(8,128)(2,1)S(1)} %get-tuple-element.7.scaled_ref), custom_call_target="tpu_custom_call" | custom-call | tf_op jit(solution)/shard_map/outputs/pallas_call | solution.py:567
  167.5 0.6 copy.9
  168.1 0.7 copy.10
Async XLA Ops:
  0.6 3.4 %copy-start = (bf16[2,256,8192]{2,1,0:T(8,128)(2,1)S(1)}, bf16[2,256,8192]{2,1,0:T(8,128)(2,1)}, u32[]{:S(2)}) copy-start(bf16[2,256,8192]{2,1,0:T(8,128)(2,1)} %acts_ref.1) | copy-start | bytes 25165828
  4.0 1.5 copy-start.1
  5.5 1.0 copy-start.2
  6.5 1.0 copy-start.3
  7.6 0.7 copy-start.4

commit v5 on v4

--- a/solution.py
+++ b/solution.py
@@ -277,7 +277,8 @@
 
 
 def chain_kernel(
-    sketch_ref, acts_ref, grads_ref, len_ref, weight_ref, y_ref, scaled_ref, send_sems, recv_sems, load_sems, x_ref, acts, f_ref, scale_ref, first, back, again, part, xgot_f, xgot_b,
+    sketch_in, acts_ref, grads_in, len_in, weight_in, y_ref, scaled_ref, send_sems, recv_sems, load_sems, sketch_ref, grads_ref, len_ref,
+    weight_ref, x_ref, acts, f_ref, scale_ref, first, back, again, part, xgot_f, xgot_b,
     xsum_f, xsum_b, projected, *scratch
 ):
     net = Net(send_sems, recv_sems)
@@ -333,16 +334,20 @@
         rings[p].gather_end()
         again[:, pl.ds(p * WIDE, WIDE)] = dot(back[...], projected[p], ((1,), (0,)))
 
-    arrived = greet(peers + [far] + xpeer)
-    loads = [pltpu.make_async_copy(acts_ref.at[n], acts.at[n], load_sems.at[n]) for n in range(2)]
+    moves = [(weight_in, weight_ref), (sketch_in, sketch_ref), (grads_in, grads_ref), (len_in, len_ref)]
+    moves += [(acts_ref.at[n], acts.at[n]) for n in range(2)]
+    loads = [pltpu.make_async_copy(a, b, load_sems.at[n]) for n, (a, b) in enumerate(moves)]
     for load in loads:
         load.start()
+    arrived = greet(peers + [far] + xpeer)
+    for load in loads[:2]:
+        load.wait()
     for n in range(4):
         at = pl.ds(n * 512, 512)
         x_ref[at, :] = dot(weight_ref[:, at], sketch_ref[...], ((0,), (0,)))
 
     def masses(n):
-        loads[n].wait()
+        loads[4 + n].wait()
         valid = lax.broadcasted_iota(jnp.int32, (COLS, LEN), 1) < len_ref[n]
         grads = jnp.where(valid, grads_ref[n].astype(F32), 0.0).astype(BF16)
         tokens = dot(grads, grads, ((0,), (0,)))
@@ -357,6 +362,8 @@
                 line = sums[:, i * 128 : (i + 1) * 128]
                 f_ref[at, :] = line if n == 0 else f_ref[at, :] + line
 
+    for load in loads[2:4]:
+        load.wait()
     masses(0)
     arrived()
     for p in range(PIECES):
@@ -378,18 +385,16 @@
     return pl.pallas_call(
         chain_kernel,
         out_shape=(jax.ShapeDtypeStruct((ROWS, RANK), BF16), jax.ShapeDtypeStruct((COLS, ROWS), BF16)),
-        in_specs=[
-            VMEM,
-            pl.BlockSpec(memory_space=pltpu.HBM),
-            VMEM,
-            pl.BlockSpec(memory_space=pltpu.SMEM),
-            VMEM,
-        ],
+        in_specs=[pl.BlockSpec(memory_space=pltpu.HBM)] * 5,
         out_specs=(VMEM, VMEM),
         scratch_shapes=[
             pltpu.SemaphoreType.DMA((copies,)),
             pltpu.SemaphoreType.DMA((copies,)),
-            pltpu.SemaphoreType.DMA((2,)),
+            pltpu.SemaphoreType.DMA((6,)),
+            pltpu.VMEM((COLS, RANK), BF16),
+            pltpu.VMEM((2, COLS, LEN), BF16),
+            pltpu.SMEM((2,), jnp.int32),
+            pltpu.VMEM((COLS, ROWS), BF16),
             pltpu.VMEM((ROWS, RANK), F32),
             pltpu.VMEM((2, LEN, DIM), BF16),
             pltpu.VMEM((64, 128), F32),
@@ -585,7 +590,8 @@
 
 
 def local(activations, out_grads, valid_len, weight, sketch):
-    second, scaled = chain(sketch, activations, out_grads.transpose(0, 2, 1), valid_len, weight.T)
+    arrays = (sketch, activations, out_grads.transpose(0, 2, 1), valid_len, weight.T)
+    second, scaled = chain(*(pltpu.with_memory_space_constraint(a, pltpu.HBM) for a in arrays))
     basis, coeffs = outputs(second, scaled)
     return basis, coeffs.T
 

time: 171 us -> 163 us (0.953)
  local copies, waits for them, and re-layouts: 8.88 us -> 1.32 us
    unnamed x12 -> x2, local copies, waits for them, and re-layouts: 8.88 us -> 1.32 us
where the time goes in v5:
time: 163 us; the launch traced here: 162 us
  Pallas kernels  160 us (98%)
    pallas_call x1, Pallas kernels, chain(): pl.pallas_call(chain_kernel, out_shape=(jax.ShapeDtypeStruct((ROWS, RANK)...  104 us
    pallas_call x1, Pallas kernels, outputs(): pl.pallas_call(tail_kernel, out_shape=(jax.ShapeDtypeStruct((32, RANK), F...  55.5 us

profile of v5, /device:TPU:6, one launch (start us, length us, event | category | flops | bytes accessed | tf_op | source)
XLA Modules:
  0.0 161.9 jit_solution(10931770383584745485)
XLA Ops:
  0.6 104.5 %chain.1 = (bf16[2048,512]{1,0:T(8,128)(2,1)S(1)}, bf16[448,2048]{1,0:T(8,128)(2,1)S(1)}) custom-call(bf16[448,512]{1,0:T(8,128)(2,1)} %sketch_in.1, bf16[2,256,8192]{2,1,0:T(8,128)(2,1)} %acts_ref.1, bf16[2,448,256]{2,1,0:T(8,128)(2,1)} %bitcast.5, s32[2]{0:T(128)} %len_in.1, bf16[448,2048]{1,0:T(8,128)(2,1)} %bitcast.4), custom_call_target="tpu_custom_call" | custom-call | tf_op jit(solution)/shard_map/chain/pallas_call | solution.py:385
  105.1 55.5 %outputs.1 = (f32[32,512]{1,0:T(8,128)S(1)}, f32[448,128]{1,0:T(8,128)S(1)}) custom-call(bf16[2048,512]{1,0:T(8,128)(2,1)S(1)} %get-tuple-element.6.y_ref, bf16[448,2048]{1,0:T(8,128)(2,1)S(1)} %get-tuple-element.7.scaled_ref), custom_call_target="tpu_custom_call" | custom-call | tf_op jit(solution)/shard_map/outputs/pallas_call | solution.py:572
  160.6 0.6 copy.9
  161.2 0.7 copy.10

commit v6 on v5

--- a/solution.py
+++ b/solution.py
@@ -427,21 +427,13 @@
     )(sketch, acts, grads, lens, weight)
 
 
-def ring_scratch(copies, front, back, width, dtype):
-    return [
-        pltpu.SemaphoreType.DMA((copies,)),
-        pltpu.SemaphoreType.DMA((copies,)),
-        pltpu.VMEM((3, front, width), dtype),
-        pltpu.VMEM((3, back, width), dtype),
-        pltpu.VMEM((front, width), dtype),
-        pltpu.VMEM((back, width), dtype),
+def exchange_scratch(rows, width, half):
+    return [pltpu.VMEM((rows, width), F32)] * 2 + [
+        pltpu.VMEM((3, half, width), F32),
+        pltpu.VMEM((3, half, width), F32),
+        pltpu.VMEM((half, width), F32),
+        pltpu.VMEM((half, width), F32),
     ]
-
-
-def row_ring(net, chunk, front):
-    row, col, _, _, _ = place()
-    up, down = (lax.rem(row + 1, 4), col), (lax.rem(row + 3, 4), col)
-    return Ring(net, row, up, down, chunk, front), [up, down]
 
 
 def unit_inverse(block):
@@ -492,61 +484,99 @@
 
 
 def tail_kernel(
-    y_ref, scaled_ref, basis_ref, coef_ref, send_sems, recv_sems, got_f, got_b, sum_f, sum_b, own, g_ref, x_ref, m_ref, part, got, whole
+    y_ref, scaled_ref, basis_ref, coef_ref, send_sems, recv_sems, x_ref, m_ref, part, got, whole, *scratch
 ):
     exact = lax.Precision.HIGHEST
     net = Net(send_sems, recv_sems)
     row, col, core, z, y = place()
     partner = (row, (y * 8 + z) * 2 + 1 - core)
-    ring, peers = row_ring(net, 64, 32)
-    far = (lax.rem(row + 2, 4), col)
-    half = core * 256
-    left = y_ref[:, pl.ds(pl.multiple_of(half, 128), 256)]
-    arrived = greet(peers + [far, partner])
-    own[...] = dot(left, y_ref[...], ((0,), (0,)))
+    up, down, far = [(lax.rem(row + d, 4), col) for d in (1, 3, 2)]
+    arrived = greet([up, down, far, partner])
+
+    def exchange(width, first, chunk, own, total, got_f, got_b, sum_f, sum_b):
+        ring, swaps = Ring(net, row, up, down, chunk, chunk // 2), []
+        base = core * 4 * chunk
+
+        def src(start, count):
+            return at_rows(own, base + start, count, 8)
+
+        def dst(start, count):
+            return at_rows(total, base + start, count, 8)
+
+        def swap(start):
+            swaps.append(net.send(dst(start, chunk), dst(start, chunk), partner))
+
+        def product():
+            side = y_ref[:, first : first + width]
+            own[...] = dot(side, y_ref[:, first:], ((0,), (0,)))
+
+        def middle():
+            top, low = ring.reduce_end(src, got_f, got_b)
+            dst(ring.own, chunk // 2)[...] = top
+            dst(ring.own + chunk // 2, chunk // 2)[...] = low
+            ring.gather_start(dst)
+            swap(ring.own)
+
+        def relay():
+            ring.gather_relay(dst)
+            swap(ring.last)
+            swap(ring.next)
+
+        def end():
+            ring.gather_end()
+            swap(ring.far)
+
+        def wait():
+            for copy in swaps:
+                copy.wait_recv()
+
+        start = functools.partial(ring.reduce_start, src, got_f, got_b)
+        turn = functools.partial(ring.reduce_relay, src, got_f, got_b, sum_f, sum_b)
+        return product, start, turn, middle, relay, end, wait
+
+    one = exchange(128, 0, 16, *scratch[:6])
+    two = exchange(384, 128, 48, *scratch[6:])
+    one[0]()
     arrived()
-    src = functools.partial(at_rows, own, step=8)
-
-    def dst(start, count):
-        return at_rows(g_ref, half + start, count, 8)
-
-    ring.reduce_start(src, got_f, got_b)
+    one[1]()
+    two[0]()
+    two[1]()
+    one[2]()
     part[...] = dot(scaled_ref[...], y_ref[...], ((1,), (0,)))
-    ring.reduce_relay(src, got_f, got_b, sum_f, sum_b)
-    top, low = ring.reduce_end(src, got_f, got_b)
-    dst(ring.own, 32)[...] = top
-    dst(ring.own + 32, 32)[...] = low
-    ring.gather_start(dst)
-    swaps = [net.send(dst(ring.own, 64), dst(ring.own, 64), partner)]
-    ring.gather_relay(dst)
-    for start in (ring.last, ring.next):
-        swaps.append(net.send(dst(start, 64), dst(start, 64), partner))
-    ring.gather_end()
-    swaps.append(net.send(dst(ring.far, 64), dst(ring.far, 64), partner))
+    for stage in (3, 4):
+        one[stage]()
+        two[stage - 1]()
+    one[5]()
+    two[4]()
+    two[5]()
 
     chunk = COLS // 4
-    xpeer = [peers[0], far, peers[1]]
+    xpeer = [up, far, down]
     for d in range(3):
         net.send(at_rows(part, lax.rem(row + d + 1, 4) * chunk, chunk), got.at[d], xpeer[d])
     scatter = net.copies[-3:]
     mine, summed = at_rows(part, row * chunk, chunk), at_rows(whole, row * chunk, chunk)
     gather = [net.make(summed, summed, peer) for peer in xpeer]
-    for copy in swaps:
-        copy.wait_recv()
-    x_ref[...] = g_ref[...]
+    one[6]()
+    corner = unit_inverse(scratch[1][:, :128])
+    two[6]()
+    x_ref[pl.ds(0, 128), :] = scratch[1][...]
+    x_ref[pl.ds(128, 384), pl.ds(128, 384)] = scratch[7][...]
 
     size = 128
     eye = lax.broadcasted_iota(jnp.int32, (size, size), 0) == lax.broadcasted_iota(jnp.int32, (size, size), 1)
 
-    def block(k, carry):
-        at = pl.ds(pl.multiple_of(k * size, size), size)
-        unit = unit_inverse(x_ref[at, at])
+    def update(k, at, unit):
         x_ref[:, at] = jnp.zeros((RANK, size), F32)
         x_ref[at, at] = eye.astype(F32)
         line = dot(unit, x_ref[at, :], ((1,), (0,)), exact)
         later = lax.broadcasted_iota(jnp.int32, (size, RANK), 1) >= (k + 1) * size
         m_ref[at, :] = jnp.where(later, 0.0, line)
         x_ref[...] = x_ref[...] - dot(jnp.where(later, line, 0.0), line, ((0,), (0,)), exact)
+
+    def block(k, carry):
+        at = pl.ds(pl.multiple_of(k * size, size), size)
+        update(k, at, unit_inverse(x_ref[at, at]))
 
         @pl.when(k == 1)
         def _():
@@ -558,7 +588,8 @@
 
         return carry
 
-    lax.fori_loop(0, RANK // size, block, 0)
+    update(0, pl.ds(0, size), corner)
+    lax.fori_loop(1, RANK // size, block, 0)
     rows = y_ref[pl.ds(pl.multiple_of(col * 32, 16), 32)].astype(F32)
     basis_ref[...] = dot(rows, m_ref[...], ((1,), (1,)), exact) * math.sqrt(DIM)
     for copy in gather:
@@ -574,16 +605,17 @@
         out_shape=(jax.ShapeDtypeStruct((32, RANK), F32), jax.ShapeDtypeStruct((COLS, RANK // 4), F32)),
         in_specs=[VMEM, VMEM],
         out_specs=(VMEM, VMEM),
-        scratch_shapes=ring_scratch(20, 32, 32, RANK, F32)
-        + [
-            pltpu.VMEM((256, RANK), F32),
-            pltpu.VMEM((RANK, RANK), F32),
+        scratch_shapes=[
+            pltpu.SemaphoreType.DMA((34,)),
+            pltpu.SemaphoreType.DMA((34,)),
             pltpu.VMEM((RANK, RANK), F32),
             pltpu.VMEM((RANK, RANK), F32),
             pltpu.VMEM((COLS, RANK), F32),
             pltpu.VMEM((3, COLS // 4, RANK), F32),
             pltpu.VMEM((COLS, RANK), F32),
-        ],
+        ]
+        + exchange_scratch(128, RANK, 8)
+        + exchange_scratch(384, 384, 24),
         compiler_params=params(3, 24),
         name="outputs",
     )(second, scaled)

time: 163 us -> 162 us (level)
  no operation moved by 1% of the time
where the time goes in v6:
time: 162 us
  Pallas kernels  160 us (99%)
    pallas_call x1, Pallas kernels, chain(): pl.pallas_call(chain_kernel, out_shape=(jax.ShapeDtypeStruct((ROWS, RANK)...  104 us
    pallas_call x1, Pallas kernels, outputs(): pl.pallas_call(tail_kernel, out_shape=(jax.ShapeDtypeStruct((32, RANK), F...  55.3 us

profile of v6, /device:TPU:6, one launch (start us, length us, event | category | flops | bytes accessed | tf_op | source)
XLA Modules:
  0.0 161.7 jit_solution(9713931829390216582)
XLA Ops:
  0.6 104.5 %chain.1 = (bf16[2048,512]{1,0:T(8,128)(2,1)S(1)}, bf16[448,2048]{1,0:T(8,128)(2,1)S(1)}) custom-call(bf16[448,512]{1,0:T(8,128)(2,1)} %sketch_in.1, bf16[2,256,8192]{2,1,0:T(8,128)(2,1)} %acts_ref.1, bf16[2,448,256]{2,1,0:T(8,128)(2,1)} %bitcast.5, s32[2]{0:T(128)} %len_in.1, bf16[448,2048]{1,0:T(8,128)(2,1)} %bitcast.4), custom_call_target="tpu_custom_call" | custom-call | tf_op jit(solution)/shard_map/chain/pallas_call | solution.py:385
  105.1 55.3 %outputs.1 = (f32[32,512]{1,0:T(8,128)S(1)}, f32[448,128]{1,0:T(8,128)S(1)}) custom-call(bf16[2048,512]{1,0:T(8,128)(2,1)S(1)} %get-tuple-element.6.y_ref, bf16[448,2048]{1,0:T(8,128)(2,1)S(1)} %get-tuple-element.7.scaled_ref), custom_call_target="tpu_custom_call" | custom-call | tf_op jit(solution)/shard_map/outputs/pallas_call | solution.py:603
  160.4 0.6 copy.9
  161.0 0.7 copy.10
